TPU v7x, 128 devices: a whole 4x4x4 slice. The times are simulated.
128 devices in a mesh: dp: 16 (over z, y), expert: 8 (over x, core).
Axes of the slice: x: 4, y: 4, z: 4, core: 2. Of those that a mesh axis runs over, the one named last changes fastest.
Arguments:
- tokens: bfloat16 [65536, 768], P(('dp', 'expert')), may hold values from -6 to 6
- assigned: int32 [65536, 1], P(('dp', 'expert')), may hold values from 0 to 7; in each aligned block of 512 rows (0 to 511, 512 to 1023, ...) at most 128 rows name the same one
- gate_prob: float32 [65536, 1], P(('dp', 'expert')), may hold values from 0.2 to 1
- cotangent: bfloat16 [65536, 768], P(('dp', 'expert')), may hold values from -6 to 6
- weight_in: bfloat16 [8, 768, 3072], P('expert'), may hold values from -0.21875 to 0.21875
- weight_out: bfloat16 [8, 3072, 768], P('expert'), may hold values from -0.109375 to 0.109375
- moment_in: float32 [8, 768, 3072], P('expert', 'dp'), may hold values from -60 to 60
- moment_out: float32 [8, 3072, 768], P('expert', 'dp'), may hold values from -60 to 60
- second_in: float32 [8, 768, 3072], P('expert', 'dp'), may hold values from 1 to 1000
- second_out: float32 [8, 3072, 768], P('expert', 'dp'), may hold values from 1 to 1000
Outputs:
- combined: bfloat16 [65536, 768], P(('dp', 'expert'))
- new_weight_in: float32 [8, 768, 3072], P('expert', 'dp')
- new_weight_out: float32 [8, 3072, 768], P('expert', 'dp')
- new_moment_in: float32 [8, 768, 3072], P('expert', 'dp')
- new_moment_out: float32 [8, 3072, 768], P('expert', 'dp')
- new_second_in: float32 [8, 768, 3072], P('expert', 'dp')
- new_second_out: float32 [8, 3072, 768], P('expert', 'dp')
Inputs may be any that keep to these rules, and one draw needn't show every extreme that they name: `assigned`: within each device's 512 rows (aligned blocks), no expert is named more than 128 times, a bound that some block reaches; every expert is named somewhere.
All inputs are finite; a program needn't handle non-finite values.
Results may differ from a plain program's by a relative error of at most 0.0012.
The roundings to bfloat16 on the way count: a program that leaves them out, or rounds other values in their place, can miss the bound.
Values may be sent and summed in bfloat16 or wider, within the bound.
A program may use at most 192 MiB of HBM per device.

v0:
```python
import jax
import jax.numpy as jnp
from jax import lax
from jax.sharding import PartitionSpec as P

eps_adasum = 1e-06


def from_partner(x, axis, bit):
    return lax.ppermute(x, axis, [(i, i ^ 1 << bit) for i in range(lax.axis_size(axis))])


def gelu_tanh(values):
    return jax.nn.gelu(values, approximate=True)


def adam_update(grad, weight, moment, second):
    new_moment = 0.9 * moment + 0.1 * grad
    new_second = 0.999 * second + 0.001 * grad * grad
    corr_one = 1.0 - 0.9**10.0
    corr_two = 1.0 - 0.999**10.0
    update = new_moment / corr_one / (jnp.sqrt(new_second / corr_two) + 1e-08)
    return (weight - 0.001 * update, new_moment, new_second)


def contract_rows(left, right):
    return lax.dot_general(
        left, right, (((0,), (0,)), ((), ())), preferred_element_type=jnp.float32
    )


def group_total(stats, bit, levels):
    summed = stats
    for other_bit in range(bit, levels):
        summed = summed + from_partner(summed, "dp", other_bit)
    return summed


def combine_level(mine, theirs, my_bit, bit, levels):
    lower = my_bit == 0
    first = jnp.where(lower, mine, theirs)
    second = jnp.where(lower, theirs, mine)
    stats = jnp.stack([jnp.sum(first * second), jnp.sum(first * first), jnp.sum(second * second)])
    totals = group_total(stats, bit, levels)
    coef_first = 1.0 - totals[0] / (2.0 * (totals[1] + eps_adasum))
    coef_second = 1.0 - totals[0] / (2.0 * (totals[2] + eps_adasum))
    return coef_first * first + coef_second * second


def body(
    tokens,
    assigned,
    gate_prob,
    cotangent,
    weight_in,
    weight_out,
    moment_in,
    moment_out,
    second_in,
    second_out,
):
    f32 = jnp.float32
    bf16 = jnp.bfloat16
    experts = lax.axis_size("expert")
    replicas = lax.axis_size("dp")
    levels = replicas.bit_length() - 1
    self_index = lax.axis_index("dp")
    tok_rows = tokens.shape[0]
    width = tokens.shape[1]
    hidden_width = weight_in.shape[2]
    capacity = 2 * tok_rows // experts
    buffer_rows = experts * capacity
    expert_ids = assigned[:, 0]
    one_hot = (expert_ids[:, None] == jnp.arange(experts, dtype=jnp.int32)[None, :]).astype(
        jnp.int32
    )
    slot_index = jnp.sum((jnp.cumsum(one_hot, axis=0) - one_hot) * one_hot, axis=1)
    slot_code = expert_ids * capacity + slot_index
    table = (jnp.arange(buffer_rows, dtype=jnp.int32)[:, None] == slot_code[None, :]).astype(bf16)
    scaled = (gate_prob * cotangent.astype(f32)).astype(bf16)
    sent_tokens = (
        jnp.dot(table, tokens, preferred_element_type=f32)
        .astype(bf16)
        .reshape(experts, capacity, width)
    )
    sent_grads = (
        jnp.dot(table, scaled, preferred_element_type=f32)
        .astype(bf16)
        .reshape(experts, capacity, width)
    )
    got_tokens, got_grads = (
        lax.all_to_all(sent_tokens, "expert", split_axis=0, concat_axis=0, tiled=True),
        lax.all_to_all(sent_grads, "expert", split_axis=0, concat_axis=0, tiled=True),
    )
    inputs = got_tokens.reshape(buffer_rows, width)
    upstream = got_grads.reshape(buffer_rows, width)
    w_first = weight_in[0]
    w_second = weight_out[0]
    pre_act = jnp.dot(inputs, w_first, preferred_element_type=f32)
    activated, gelu_back = jax.vjp(gelu_tanh, pre_act)
    hidden = activated.astype(bf16)
    expert_out = (
        jnp.dot(hidden, w_second, preferred_element_type=f32)
        .astype(bf16)
        .reshape(experts, capacity, width)
    )
    returned = lax.all_to_all(expert_out, "expert", split_axis=0, concat_axis=0, tiled=True)
    picked = contract_rows(table, returned.reshape(buffer_rows, width))
    combined = (gate_prob * picked).astype(bf16)
    back_in = lax.dot_general(
        upstream, w_second, (((1,), (1,)), ((), ())), preferred_element_type=f32
    )
    hidden_grad = gelu_back(back_in)[0].astype(bf16)
    grad_in = contract_rows(inputs, hidden_grad)
    grad_out = contract_rows(hidden, upstream)
    vectors = jnp.stack([grad_in.reshape(-1, 128), grad_out.reshape(-1, 128)])
    for bit in range(levels - 1, -1, -1):
        my_bit = self_index >> bit & 1
        half_count = vectors.shape[1] // 2
        kept = lax.dynamic_slice_in_dim(vectors, my_bit * half_count, half_count, 1)
        outgoing = lax.dynamic_slice_in_dim(vectors, (1 - my_bit) * half_count, half_count, 1)
        incoming = from_partner(outgoing, "dp", bit)
        vectors = combine_level(kept, incoming, my_bit, bit, levels)
    rows_first = width // replicas
    rows_second = hidden_width // replicas
    seg_first = vectors[0].reshape(rows_first, hidden_width)
    seg_second = vectors[1].reshape(rows_second, width)
    own_first = lax.dynamic_slice_in_dim(w_first, self_index * rows_first, rows_first, 0).astype(
        f32
    )
    own_second = lax.dynamic_slice_in_dim(
        w_second, self_index * rows_second, rows_second, 0
    ).astype(f32)
    new_w_first, new_m_first, new_v_first = adam_update(
        seg_first, own_first, moment_in[0], second_in[0]
    )
    new_w_second, new_m_second, new_v_second = adam_update(
        seg_second, own_second, moment_out[0], second_out[0]
    )
    return (
        combined,
        new_w_first[None],
        new_w_second[None],
        new_m_first[None],
        new_m_second[None],
        new_v_first[None],
        new_v_second[None],
    )


def solution(mesh):
    return jax.shard_map(
        body,
        mesh=mesh,
        in_specs=(
            P(("dp", "expert"), None),
            P(("dp", "expert"), None),
            P(("dp", "expert"), None),
            P(("dp", "expert"), None),
            P("expert", None, None),
            P("expert", None, None),
            P("expert", "dp", None),
            P("expert", "dp", None),
            P("expert", "dp", None),
            P("expert", "dp", None),
        ),
        out_specs=(
            P(("dp", "expert"), None),
            P("expert", "dp", None),
            P("expert", "dp", None),
            P("expert", "dp", None),
            P("expert", "dp", None),
            P("expert", "dp", None),
            P("expert", "dp", None),
        ),
        check_vma=False,
    )
```

profile of v0, /device:TPU:0, one launch (start us, length us, event | category | flops | bytes accessed | tf_op | source)
XLA Modules:
  0.0 627.5 jit_solution(12079451678568266763)
XLA Ops:
  4.3 2.2 fusion.20
  6.5 4.4 all-to-all-start
  10.9 2.3 fusion.21
  13.2 19.2 %all-to-all-done = bf16[8,128,768]{2,1,0:T(8,128)(2,1)S(1)} async-done(((bf16[8,128,768]{2,1,0:T(8,128)(2,1)}), bf16[8,128,768]{2,1,0:T(8,128)(2,1)S(1)}, u32[]{:S(2)}, u32[]{:S(2)}) %all-to-all-start) | async-done | bytes 1572896 | tf_op jit(solution)/shard_map/all_to_all | solution.py:92
  32.5 4.5 all-to-all-start.2
  37.0 10.3 %fusion.15 = f32[1024,3072]{1,0:T(8,128)} fusion(bf16[1024,768]{1,0:T(8,128)(2,1)S(1)} %bitcast.55, bf16[1,768,3072]{2,1,0:T(8,128)(2,1)} %param.14), kind=kOutput, calls=%fused_computation.21 | convolution fusion | flops 4831838208 | bytes 18874368 | tf_op jit(solution)/shard_map/dot_general | solution.py:99
  47.3 11.1 %all-to-all-done.2 = bf16[8,128,768]{2,1,0:T(8,128)(2,1)} async-done(((bf16[8,128,768]{2,1,0:T(8,128)(2,1)}), bf16[8,128,768]{2,1,0:T(8,128)(2,1)}, u32[]{:S(2)}, u32[]{:S(2)}) %all-to-all-start.2) | async-done | bytes 1572896 | tf_op jit(solution)/shard_map/all_to_all | solution.py:93
  58.3 12.8 %fusion.40 = f32[3072,768]{1,0:T(8,128)} fusion(bf16[1024,768]{1,0:T(8,128)(2,1)} %bitcast.12, f32[1024,3072]{1,0:T(8,128)} %fusion.15), kind=kOutput, calls=%fused_computation.86 | convolution fusion | flops 4860149760 | bytes 23592960 | tf_op jit(solution)/shard_map/dot_general | solution.py:27
  71.1 19.1 %fusion.7 = f32[768,3072]{1,0:T(8,128)} fusion(bf16[1024,768]{1,0:T(8,128)(2,1)S(1)} %bitcast.56, f32[1024,3072]{1,0:T(8,128)} %fusion.15, bf16[1024,768]{1,0:T(8,128)(2,1)} %bitcast.12, bf16[1,3072,768]{2,1,0:T(8,128)(2,1)} %param.15), kind=kOutput, calls=%fused_computation.16 | convolution fusion | flops 9726590976 | bytes 29884416 | tf_op jit(solution)/shard_map/dot_general | solution.py:27
  90.2 10.9 %stack_reshape.6 = f32[1,18432,128]{2,1,0:T(8,128)} reshape(f32[768,3072]{1,0:T(8,128)} %fusion.7) | data formatting | bytes 18874368 | tf_op jit(solution)/shard_map/stack;reshape | solution.py:116
  101.1 8.3 %constant_dynamic-update-slice_fusion.1 = f32[2,18432,128]{2,1,0:T(8,128)} fusion(f32[1,18432,128]{2,1,0:T(8,128)} %stack_reshape.6), kind=kLoop, calls=%fused_computation.70 | loop fusion | bytes 18874368
  109.5 10.7 %stack_reshape.7 = f32[1,18432,128]{2,1,0:T(8,128)} reshape(f32[3072,768]{1,0:T(8,128)} %fusion.40) | data formatting | bytes 18874368 | tf_op jit(solution)/shard_map/stack;reshape | solution.py:116
  120.2 8.3 %constant_dynamic-update-slice_fusion = f32[2,18432,128]{2,1,0:T(8,128)} fusion(f32[2,18432,128]{2,1,0:T(8,128)} %constant_dynamic-update-slice_fusion.1, f32[1,18432,128]{2,1,0:T(8,128)} %stack_reshape.7), kind=kLoop, calls=%fused_computation.69 | loop fusion | bytes 18874368 | tf_op jit(solution)/shard_map/stack | solution.py:116
  128.5 6.4 %constant_dynamic-slice_fusion.3 = f32[2,9216,128]{2,1,0:T(8,128)} fusion(f32[2,18432,128]{2,1,0:T(8,128)} %constant_dynamic-update-slice_fusion, s32[]{:T(128)S(6)} %select_n.84), kind=kLoop, calls=%fused_computation.74 | loop fusion | bytes 18874372 | tf_op jit(solution)/shard_map/dynamic_slice | solution.py:121
  134.9 3.9 collective-permute-start
  138.8 202.9 %collective-permute-done = f32[2,9216,128]{2,1,0:T(8,128)} collective-permute-done((f32[2,9216,128]{2,1,0:T(8,128)}, f32[2,9216,128]{2,1,0:T(8,128)}, u32[]{:S(2)}, u32[]{:S(2)}) %collective-permute-start) | collective-permute-done | bytes 9437216 | tf_op jit(solution)/shard_map/ppermute | solution.py:10
  341.8 8.1 %multiply_reduce_fusion.2 = (f32[]{:T(128)}, f32[]{:T(128)}, f32[]{:T(128)}, f32[2,9216,128]{2,1,0:T(8,128)S(1)}, f32[2,9216,128]{2,1,0:T(8,128)S(1)}) fusion(f32[2,9216,128]{2,1,0:T(8,128)} %collective-permute-done, f32[2,18432,128]{2,1,0:T(8,128)} %constant_dynamic-update-slice_fusion, s32[]{:T(128)S(6)} %select_n.83, pred[]{:T(512)S(6)} %eq.61), kind=kLoop, calls=%fused_computation.13 | loop fusion | flops 18874364 | bytes 37748752 | tf_op jit(solution)/shard_map/reduce_sum | solution.py:43
  351.9 3.3 collective-permute-start.1
  357.0 2.0 fusion.57
  362.2 4.1 multiply_add_fusion
  366.4 4.8 constant_dynamic-slice_fusion.2
  372.4 100.5 %collective-permute-done.2 = f32[2,4608,128]{2,1,0:T(8,128)} collective-permute-done((f32[2,4608,128]{2,1,0:T(8,128)}, f32[2,4608,128]{2,1,0:T(8,128)}, u32[]{:S(2)}, u32[]{:S(2)}) %collective-permute-start.2) | collective-permute-done | bytes 4718624 | tf_op jit(solution)/shard_map/ppermute | solution.py:10
  473.0 5.1 multiply_reduce_fusion.5
  481.2 2.6 collective-permute-done.3
  485.7 3.0 collective-permute-start.4
  488.7 2.1 collective-permute-done.4
  490.8 2.0 fusion.60
  496.8 3.3 collective-permute-start.5
  500.1 11.3 %fusion.22 = bf16[1024,768]{1,0:T(8,128)(2,1)} fusion(bf16[1,3072,768]{2,1,0:T(8,128)(2,1)S(1)} %bitcast.60, f32[1024,3072]{1,0:T(8,128)} %fusion.15), kind=kOutput, calls=%fused_computation.41 | convolution fusion | flops 4860936192 | bytes 18874368 | tf_op jit(solution)/shard_map/dot_general | solution.py:103
  511.3 4.3 all-to-all-start.1
  515.6 30.6 %collective-permute-done.5 = f32[2,2304,128]{2,1,0:T(8,128)} collective-permute-done((f32[2,2304,128]{2,1,0:T(8,128)S(1)}, f32[2,2304,128]{2,1,0:T(8,128)}, u32[]{:S(2)}, u32[]{:S(2)}) %collective-permute-start.5) | collective-permute-done | bytes 2359328 | tf_op jit(solution)/shard_map/ppermute | solution.py:10
  546.3 3.6 multiply_reduce_fusion.8
  551.9 3.2 collective-permute-start.6
  559.8 2.8 collective-permute-done.7
  562.6 2.0 fusion.59
  564.6 2.7 collective-permute-start.8
  567.3 2.4 collective-permute-done.8
  575.8 3.5 multiply_convert_fusion.2
  579.3 13.5 %collective-permute-done.9 = f32[2,1152,128]{2,1,0:T(8,128)} collective-permute-done((f32[2,1152,128]{2,1,0:T(8,128)}, f32[2,1152,128]{2,1,0:T(8,128)}, u32[]{:S(2)}, u32[]{:S(2)}) %collective-permute-start.9) | collective-permute-done | bytes 1179680 | tf_op jit(solution)/shard_map/ppermute | solution.py:10
  592.8 2.2 multiply_reduce_fusion.11
  595.0 2.1 pad_maximum_fusion.3
  602.7 3.2 collective-permute-start.11
  607.8 2.0 fusion.58
  610.3 3.1 collective-permute-done.12
  613.4 2.4 collective-permute-start.13
  615.8 2.7 collective-permute-done.13
  622.1 2.6 multiply_subtract_fusion.1
  624.7 2.8 multiply_subtract_fusion
  (56 shorter events, 34.9 us)
Async XLA Ops:
  0.6 3.7 copy-start
  0.6 10.3 %copy-start.5 = (f32[512,1]{0,1:T(1,128)S(1)}, f32[512,1]{0,1:T(1,128)}, u32[]{:S(2)}) copy-start(f32[512,1]{0,1:T(1,128)} %param.12) | copy-start | bytes 6148
  0.7 10.3 %copy-start.4 = (bf16[512,768]{1,0:T(8,128)(2,1)S(1)}, bf16[512,768]{1,0:T(8,128)(2,1)}, u32[]{:S(2)}) copy-start(bf16[512,768]{1,0:T(8,128)(2,1)} %param.13) | copy-start | bytes 2359300
  6.5 26.0 %all-to-all-start = ((bf16[8,128,768]{2,1,0:T(8,128)(2,1)}), bf16[8,128,768]{2,1,0:T(8,128)(2,1)S(1)}, u32[]{:S(2)}, u32[]{:S(2)}) async-start(bf16[8,128,768]{2,1,0:T(8,128)(2,1)} %bitcast.58), calls=%async_computation | async-start | bytes 3145728 | tf_op jit(solution)/shard_map/all_to_all | solution.py:92
  32.5 25.9 %all-to-all-start.2 = ((bf16[8,128,768]{2,1,0:T(8,128)(2,1)}), bf16[8,128,768]{2,1,0:T(8,128)(2,1)}, u32[]{:S(2)}, u32[]{:S(2)}) async-start(bf16[8,128,768]{2,1,0:T(8,128)(2,1)} %bitcast.57), calls=%async_computation.2 | async-start | bytes 3145728 | tf_op jit(solution)/shard_map/all_to_all | solution.py:93
  134.9 206.8 %collective-permute-start = (f32[2,9216,128]{2,1,0:T(8,128)}, f32[2,9216,128]{2,1,0:T(8,128)}, u32[]{:S(2)}, u32[]{:S(2)}) collective-permute-start(f32[2,9216,128]{2,1,0:T(8,128)} %constant_dynamic-slice_fusion.3), channel_id=1, source_target_pairs={{0,64},{8,72},{16,80},{24,88},{32,96},{40,104},{48,112},{56,120},{... | collective-permute-start | bytes 28311560 | tf_op jit(solution)/shard_map/ppermute | solution.py:10
  351.9 5.1 collective-permute-start.1
  371.1 101.8 %collective-permute-start.2 = (f32[2,4608,128]{2,1,0:T(8,128)}, f32[2,4608,128]{2,1,0:T(8,128)}, u32[]{:S(2)}, u32[]{:S(2)}) collective-permute-start(f32[2,4608,128]{2,1,0:T(8,128)} %constant_dynamic-slice_fusion.2), channel_id=1, source_target_pairs={{0,32},{8,40},{16,48},{24,56},{32,0},{40,8},{48,16},{56,24},{64,96... | collective-permute-start | bytes 14155784 | tf_op jit(solution)/shard_map/ppermute | solution.py:10
  473.0 27.1 %slice-start = ((s8[4718592]{0:T(1024)(128)(4,1)}), s8[4194304]{0:T(1024)(128)(4,1)S(1)}, s32[]{:S(2)}) async-start(s8[4718592]{0:T(1024)(128)(4,1)} %bitcast.59), calls=%async_computation.3 | async-start | bytes 8388608
  480.1 3.6 collective-permute-start.3
  485.7 5.1 collective-permute-start.4
  493.4 6.6 %slice-start.1 = ((s8[4718592]{0:T(1024)(128)(4,1)}), s8[524288]{0:T(1024)(128)(4,1)S(1)}, s32[]{:S(2)}) async-start(s8[4718592]{0:T(1024)(128)(4,1)} %bitcast.59), calls=%async_computation.4 | async-start | bytes 1048576
  496.6 14.7 %copy-start.2 = (f32[2,4608,128]{2,1,0:T(8,128)}, f32[2,4608,128]{2,1,0:T(8,128)S(1)}, u32[]{:S(2)}) copy-start(f32[2,4608,128]{2,1,0:T(8,128)S(1)} %multiply_add_fusion.1) | copy-start | bytes 14155780
  496.8 49.5 %collective-permute-start.5 = (f32[2,2304,128]{2,1,0:T(8,128)S(1)}, f32[2,2304,128]{2,1,0:T(8,128)}, u32[]{:S(2)}, u32[]{:S(2)}) collective-permute-start(f32[2,2304,128]{2,1,0:T(8,128)S(1)} %constant_dynamic-slice_fusion.1), channel_id=1, source_target_pairs={{0,16},{8,24},{16,0},{24,8},{32,48},{40,56},{48,32},{56,40},{64,80... | collective-permute-start | bytes 7077896 | tf_op jit(solution)/shard_map/ppermute | solution.py:10
  511.3 64.5 %all-to-all-start.1 = ((bf16[8,128,768]{2,1,0:T(8,128)(2,1)}), bf16[8,128,768]{2,1,0:T(8,128)(2,1)}, u32[]{:S(2)}, u32[]{:S(2)}) async-start(bf16[8,128,768]{2,1,0:T(8,128)(2,1)} %bitcast.54), calls=%async_computation.1 | async-start | bytes 3145728 | tf_op jit(solution)/shard_map/all_to_all | solution.py:107
  551.9 5.1 collective-permute-start.6
  559.0 3.6 collective-permute-start.7
  564.6 5.1 collective-permute-start.8
  574.3 18.5 %collective-permute-start.9 = (f32[2,1152,128]{2,1,0:T(8,128)}, f32[2,1152,128]{2,1,0:T(8,128)}, u32[]{:S(2)}, u32[]{:S(2)}) collective-permute-start(f32[2,1152,128]{2,1,0:T(8,128)} %constant_dynamic-slice_fusion), channel_id=1, source_target_pairs={{0,8},{8,0},{16,24},{24,16},{32,40},{40,32},{48,56},{56,48},{64,72... | collective-permute-start | bytes 3538952 | tf_op jit(solution)/shard_map/ppermute | solution.py:10
  595.0 27.1 %copy-start.3 = (f32[1,48,3072]{2,1,0:T(8,128)S(1)}, f32[1,48,3072]{2,1,0:T(8,128)}, u32[]{:S(2)}) copy-start(f32[1,48,3072]{2,1,0:T(8,128)} %param.16) | copy-start | bytes 1769476
  597.1 3.6 collective-permute-start.10
  602.7 5.1 collective-permute-start.11
  609.8 3.6 collective-permute-start.12
  613.4 5.1 collective-permute-start.13
  621.9 5.6 copy-start.1
where the time goes:
time: 629 us; the launch traced here: 628 us
  waiting for transfers between devices  401 us (64%)
  matrix products  61.5 us (10%)
  other arithmetic  55.1 us (9%)
  local copies, waits for them, and re-layouts  53.7 us (9%)
  starting transfers between devices  44.9 us (7%)
  between operations  11.3 us (2%)
    ppermute x14, waiting for transfers between devices, from_partner(): lax.ppermute(x, axis, [(i, i ^ 1 << bit) for i in range(lax.axis_size(axi...  371 us
    dot_general x3, matrix products, contract_rows(): lax.dot_general(left, right, (((0,), (0,)), ((), ())), preferred_element_...  35.4 us
    ppermute x14, starting transfers between devices, from_partner(): lax.ppermute(x, axis, [(i, i ^ 1 << bit) for i in range(lax.axis_size(axi...  31.7 us
    another operation x3, local copies, waits for them, and re-layouts, body(): vectors = jnp.stack([grad_in.reshape(-1, 128), grad_out.reshape(-1, 128)])  29.9 us
    all_to_all x1, waiting for transfers between devices, body(): lax.all_to_all(sent_tokens, 'expert', split_axis=0, concat_axis=0, tiled=...  19.2 us
    reduce_sum x4, other arithmetic, combine_level(): jnp.sum(first * second)  19.1 us
    add x10, other arithmetic, group_total(): summed = summed + from_partner(summed, 'dp', other_bit)  14.1 us
  transfers between devices with their start and end apart: 17, of which 16 were waited for; matrix products, arithmetic and copies ran while one was open for 6% of the time, Pallas kernels for 0%

commit v1 on v0

v1 whole, which is shorter than its diff:
```python
import jax
import jax.numpy as jnp
from jax import lax
from jax.sharding import PartitionSpec as P

eps_adasum = 1e-06
SIDE = 4


def shift_z(x, step):
    side = SIDE
    return lax.ppermute(
        x,
        "dp",
        [(i, (i // side + step) % side * side + i % side) for i in range(side * side)],
    )


def gelu_tanh(values):
    return jax.nn.gelu(values, approximate=True)


def adam_update(grad, weight, moment, second):
    new_moment = 0.9 * moment + 0.1 * grad
    new_second = 0.999 * second + 0.001 * grad * grad
    corr_one = 1.0 - 0.9**10.0
    corr_two = 1.0 - 0.999**10.0
    update = new_moment / corr_one / (jnp.sqrt(new_second / corr_two) + 1e-08)
    return (weight - 0.001 * update, new_moment, new_second)


def contract_rows(left, right):
    return lax.dot_general(
        left, right, (((0,), (0,)), ((), ())), preferred_element_type=jnp.float32
    )


def pair_coefs(ab, aa, bb):
    return 1.0 - ab / (2.0 * (aa + eps_adasum)), 1.0 - ab / (2.0 * (bb + eps_adasum))


def tree_weights(gram):
    w0, w2 = pair_coefs(gram[0, 2], gram[0, 0], gram[2, 2])
    w1, w3 = pair_coefs(gram[1, 3], gram[1, 1], gram[3, 3])
    aa = w0 * w0 * gram[0, 0] + 2.0 * w0 * w2 * gram[0, 2] + w2 * w2 * gram[2, 2]
    bb = w1 * w1 * gram[1, 1] + 2.0 * w1 * w3 * gram[1, 3] + w3 * w3 * gram[3, 3]
    ab = w0 * (w1 * gram[0, 1] + w3 * gram[0, 3]) + w2 * (w1 * gram[2, 1] + w3 * gram[2, 3])
    u, v = pair_coefs(ab, aa, bb)
    return jnp.stack([u * w0, v * w1, u * w2, v * w3])


def local_gram(vectors):
    rows = []
    for i in range(4):
        rows.append([None] * 4)
    for i in range(4):
        for j in range(i, 4):
            s = sum(jnp.sum(a * b) for a, b in zip(vectors[i], vectors[j]))
            rows[i][j] = s
            rows[j][i] = s
    return jnp.stack([jnp.stack(r) for r in rows])


def expert_grads(rows, upstream, w_first, w_second):
    pre_act = jnp.dot(rows, w_first, preferred_element_type=jnp.float32)
    activated, gelu_back = jax.vjp(gelu_tanh, pre_act)
    hidden = activated.astype(jnp.bfloat16)
    back_in = lax.dot_general(
        upstream, w_second, (((1,), (1,)), ((), ())), preferred_element_type=jnp.float32
    )
    hidden_grad = gelu_back(back_in)[0].astype(jnp.bfloat16)
    return contract_rows(rows, hidden_grad), contract_rows(hidden, upstream)


def body(
    tokens,
    assigned,
    gate_prob,
    cotangent,
    weight_in,
    weight_out,
    moment_in,
    moment_out,
    second_in,
    second_out,
):
    f32 = jnp.float32
    bf16 = jnp.bfloat16
    side = SIDE
    experts = lax.axis_size("expert")
    replicas = lax.axis_size("dp")
    self_index = lax.axis_index("dp")
    z_index = self_index // side
    tok_rows = tokens.shape[0]
    width = tokens.shape[1]
    hidden_width = weight_in.shape[2]
    part = hidden_width // side
    capacity = 2 * tok_rows // experts
    buffer_rows = experts * capacity
    expert_ids = assigned[:, 0]
    one_hot = (expert_ids[:, None] == jnp.arange(experts, dtype=jnp.int32)[None, :]).astype(
        jnp.int32
    )
    slot_index = jnp.sum((jnp.cumsum(one_hot, axis=0) - one_hot) * one_hot, axis=1)
    slot_code = expert_ids * capacity + slot_index
    table = (jnp.arange(buffer_rows, dtype=jnp.int32)[:, None] == slot_code[None, :]).astype(bf16)
    scaled = (gate_prob * cotangent.astype(f32)).astype(bf16)

    def to_experts(x):
        sent = jnp.dot(table, x, preferred_element_type=f32).astype(bf16)
        got = lax.all_to_all(
            sent.reshape(experts, capacity, width), "expert", split_axis=0, concat_axis=0, tiled=True
        )
        return got.reshape(buffer_rows, width)

    rows_own = to_experts(tokens)
    up_own = to_experts(scaled)
    rows_lo = shift_z(rows_own, 1)
    rows_hi = shift_z(rows_own, -1)
    up_lo = shift_z(up_own, 1)
    up_hi = shift_z(up_own, -1)
    rows_far = shift_z(rows_lo, 1)
    up_far = shift_z(up_hi, -1)

    w_first = weight_in[0]
    w_second = weight_out[0]
    w_first_part = lax.dynamic_slice_in_dim(w_first, z_index * part, part, 1)
    w_second_part = lax.dynamic_slice_in_dim(w_second, z_index * part, part, 0)

    pre_act = jnp.dot(rows_own, w_first, preferred_element_type=f32)
    hidden = gelu_tanh(pre_act).astype(bf16)
    expert_out = (
        jnp.dot(hidden, w_second, preferred_element_type=f32)
        .astype(bf16)
        .reshape(experts, capacity, width)
    )
    returned = lax.all_to_all(expert_out, "expert", split_axis=0, concat_axis=0, tiled=True)
    picked = contract_rows(table, returned.reshape(buffer_rows, width))
    combined = (gate_prob * picked).astype(bf16)

    vectors = [
        expert_grads(rows, up, w_first_part, w_second_part)
        for rows, up in (
            (rows_own, up_own),
            (rows_hi, up_hi),
            (rows_far, up_far),
            (rows_lo, up_lo),
        )
    ]
    place = (jnp.arange(side)[:, None] == (jnp.arange(side)[None, :] + z_index) % side).astype(f32)
    near = local_gram(vectors)
    gram = jnp.sum(
        place[:, None, :, None] * place[None, :, None, :] * near[None, None], axis=(2, 3)
    )
    gram = gram + shift_z(gram, 2)
    gram = gram + shift_z(gram, 1)
    weights = tree_weights(gram)
    weights = jnp.sum(place * weights[:, None], axis=0)
    comb_in = sum(weights[k] * vectors[k][0] for k in range(side))
    comb_out = sum(weights[k] * vectors[k][1] for k in range(side))

    rows_first = width // replicas
    rows_second = hidden_width // replicas
    got_in = lax.all_to_all(
        comb_in.reshape(replicas, rows_first, part), "dp", split_axis=0, concat_axis=0, tiled=True
    ).reshape(side, side, rows_first, part)
    groups = [[z * side + y for y in range(side)] for z in range(side)]
    got_out = lax.all_to_all(
        comb_out.reshape(side, rows_second, width),
        "dp",
        split_axis=0,
        concat_axis=0,
        tiled=True,
        axis_index_groups=groups,
    )
    ys = [
        (jnp.concatenate([got_in[z, y] for z in range(side)], axis=1), got_out[y])
        for y in range(side)
    ]
    gram_y = local_gram(ys)
    for bit in range(4):
        gram_y = gram_y + lax.ppermute(gram_y, "dp", [(i, i ^ 1 << bit) for i in range(replicas)])
    weights_y = tree_weights(gram_y)
    seg_first = sum(weights_y[k] * ys[k][0] for k in range(side))
    seg_second = sum(weights_y[k] * ys[k][1] for k in range(side))

    own_first = lax.dynamic_slice_in_dim(w_first, self_index * rows_first, rows_first, 0).astype(
        f32
    )
    own_second = lax.dynamic_slice_in_dim(
        w_second, self_index * rows_second, rows_second, 0
    ).astype(f32)
    new_w_first, new_m_first, new_v_first = adam_update(
        seg_first, own_first, moment_in[0], second_in[0]
    )
    new_w_second, new_m_second, new_v_second = adam_update(
        seg_second, own_second, moment_out[0], second_out[0]
    )
    return (
        combined,
        new_w_first[None],
        new_w_second[None],
        new_m_first[None],
        new_m_second[None],
        new_v_first[None],
        new_v_second[None],
    )


def solution(mesh):
    return jax.shard_map(
        body,
        mesh=mesh,
        in_specs=(
            P(("dp", "expert"), None),
            P(("dp", "expert"), None),
            P(("dp", "expert"), None),
            P(("dp", "expert"), None),
            P("expert", None, None),
            P("expert", None, None),
            P("expert", "dp", None),
            P("expert", "dp", None),
            P("expert", "dp", None),
            P("expert", "dp", None),
        ),
        out_specs=(
            P(("dp", "expert"), None),
            P("expert", "dp", None),
            P("expert", "dp", None),
            P("expert", "dp", None),
            P("expert", "dp", None),
            P("expert", "dp", None),
            P("expert", "dp", None),
        ),
        check_vma=False,
    )
```

time: 629 us -> 388 us (0.62)
  waiting for transfers between devices: 401 us -> 144 us
  local copies, waits for them, and re-layouts: 53.7 us -> 11.8 us
  matrix products: 61.5 us -> 101 us
  between operations: 11.3 us -> 49.2 us
  other arithmetic: 55.1 us -> 34.8 us
    ppermute x14 -> x12, waiting for transfers between devices: 371 us -> 77.6 us  [the longest x8 65.3 us: shift_z(): lax.ppermute(x, 'dp', [(i, (i // side + step) % side * side + i % side) f...]
    all_to_all x2 -> x4, waiting for transfers between devices: 30.3 us -> 66.8 us  [the longest x2 38.8 us: to_experts(): lax.all_to_all(sent.reshape(experts, capacity, width), 'expert', split_ax...]
    another operation x6 -> x1, local copies, waits for them, and re-layouts: 30.2 us -> 0.01 us  [the longest x3 29.9 us: body(): vectors = jnp.stack([grad_in.reshape(-1, 128), grad_out.reshape(-1, 128)])]
    dot_general x3 -> x9, matrix products: 35.4 us -> 64.9 us  [contract_rows(): lax.dot_general(left, right, (((0,), (0,)), ((), ())), preferred_element_...]
    ppermute x14 -> x12, starting transfers between devices: 31.7 us -> 17.6 us  [the longest x8 15.6 us: shift_z(): lax.ppermute(x, 'dp', [(i, (i // side + step) % side * side + i % side) f...]
    dynamic_slice x4 -> x0, local copies, waits for them, and re-layouts: 12.5 us -> none  [body(): lax.dynamic_slice_in_dim(vectors, (1 - my_bit) * half_count, half_count, 1)]
    reduce_sum x4 -> x7, other arithmetic: 19.1 us -> 8.25 us  [the longest x5 7.97 us: local_gram(): s = sum((jnp.sum(a * b) for a, b in zip(vectors[i], vectors[j])))]
    all_to_all x2 -> x4, starting transfers between devices: 8.89 us -> 17.6 us  [the longest x2 8.72 us: to_experts(): lax.all_to_all(sent.reshape(experts, capacity, width), 'expert', split_ax...]
  transfers between devices with their start and end apart: 17 -> 17, of which waited for: 16 -> 13; matrix products, arithmetic and copies ran while one was open for 6% -> 23% of each run, Pallas kernels for 0% -> 0%
where the time goes in v1:
time: 388 us; the launch traced here: 381 us
  waiting for transfers between devices  144 us (37%)
  matrix products  101 us (26%)
  between operations  49.2 us (13%)
  starting transfers between devices  39.5 us (10%)
  other arithmetic  34.8 us (9%)
  local copies, waits for them, and re-layouts  11.8 us (3%)
    ppermute x8, waiting for transfers between devices, shift_z(): lax.ppermute(x, 'dp', [(i, (i // side + step) % side * side + i % side) f...  65.3 us
    dot_general x9, matrix products, contract_rows(): lax.dot_general(left, right, (((0,), (0,)), ((), ())), preferred_element_...  64.9 us
    all_to_all x2, waiting for transfers between devices, to_experts(): lax.all_to_all(sent.reshape(experts, capacity, width), 'expert', split_ax...  38.8 us
    dot_general x4, matrix products, expert_grads(): pre_act = jnp.dot(rows, w_first, preferred_element_type=jnp.float32)  16.2 us
    all_to_all x1, waiting for transfers between devices, body(): lax.all_to_all(comb_out.reshape(side, rows_second, width), 'dp', split_ax...  16.2 us
    dot_general x1, matrix products, body(): jnp.dot(hidden, w_second, preferred_element_type=f32).astype(bf16)  15.6 us
    ppermute x8, starting transfers between devices, shift_z(): lax.ppermute(x, 'dp', [(i, (i // side + step) % side * side + i % side) f...  15.6 us
    ppermute x4, waiting for transfers between devices, body(): lax.ppermute(gram_y, 'dp', [(i, i ^ 1 << bit) for i in range(replicas)])  12.2 us
  transfers between devices with their start and end apart: 17, of which 13 were waited for; matrix products, arithmetic and copies ran while one was open for 23% of the time, Pallas kernels for 0%

profile of v1, /device:TPU:0, one launch (start us, length us, event | category | flops | bytes accessed | tf_op | source)
XLA Modules:
  0.0 380.9 jit_solution(357785283051643475)
XLA Ops:
  4.3 2.2 fusion.48
  6.5 4.4 %all-to-all-start = ((bf16[8,128,768]{2,1,0:T(8,128)(2,1)}), bf16[8,128,768]{2,1,0:T(8,128)(2,1)S(1)}, u32[]{:S(2)}, u32[]{:S(2)}) async-start(bf16[8,128,768]{2,1,0:T(8,128)(2,1)} %bitcast.5), calls=%async_computation | async-start | bytes 3145728 | tf_op jit(solution)/shard_map/all_to_all | solution.py:111
  10.9 2.3 fusion.49
  13.2 19.2 %all-to-all-done = bf16[8,128,768]{2,1,0:T(8,128)(2,1)S(1)} async-done(((bf16[8,128,768]{2,1,0:T(8,128)(2,1)}), bf16[8,128,768]{2,1,0:T(8,128)(2,1)S(1)}, u32[]{:S(2)}, u32[]{:S(2)}) %all-to-all-start) | async-done | bytes 1572896 | tf_op jit(solution)/shard_map/all_to_all | solution.py:111
  32.4 4.3 %all-to-all-start.2 = ((bf16[8,128,768]{2,1,0:T(8,128)(2,1)}), bf16[8,128,768]{2,1,0:T(8,128)(2,1)}, u32[]{:S(2)}, u32[]{:S(2)}) async-start(bf16[8,128,768]{2,1,0:T(8,128)(2,1)} %bitcast.11), calls=%async_computation.2 | async-start | bytes 3145728 | tf_op jit(solution)/shard_map/all_to_all | solution.py:111
  36.7 2.0 collective-permute-start.2
  38.7 19.6 %all-to-all-done.2 = bf16[8,128,768]{2,1,0:T(8,128)(2,1)} async-done(((bf16[8,128,768]{2,1,0:T(8,128)(2,1)}), bf16[8,128,768]{2,1,0:T(8,128)(2,1)}, u32[]{:S(2)}, u32[]{:S(2)}) %all-to-all-start.2) | async-done | bytes 1572896 | tf_op jit(solution)/shard_map/all_to_all | solution.py:111
  58.3 4.0 %collective-permute-start.1 = (bf16[1024,768]{1,0:T(8,128)(2,1)}, bf16[1024,768]{1,0:T(8,128)(2,1)}, u32[]{:S(2)}, u32[]{:S(2)}) collective-permute-start(bf16[1024,768]{1,0:T(8,128)(2,1)} %bitcast.12), channel_id=1, source_target_pairs={{0,96},{8,104},{16,112},{24,120},{32,0},{40,8},{48,16},{56,24},{64... | collective-permute-start | bytes 4718600 | tf_op jit(solution)/shard_map/ppermute | solution.py:12
  62.7 1.7 collective-permute-start.5
  64.4 4.3 %fusion.91 = f32[1024,768]{1,0:T(8,128)} fusion(bf16[1024,768]{1,0:T(8,128)(2,1)S(1)} %bitcast.221, bf16[1,768,3072]{2,1,0:T(8,128)(2,1)} %param.14, s32[]{:T(128)S(6)} %select_n.29), kind=kOutput, calls=%fused_computation.114 | convolution fusion | flops 1207959552 | bytes 5898244 | tf_op jit(solution)/shard_map/dot_general | solution.py:65
  68.7 7.4 %collective-permute-done.2 = bf16[1024,768]{1,0:T(8,128)(2,1)} collective-permute-done((bf16[1024,768]{1,0:T(8,128)(2,1)S(1)}, bf16[1024,768]{1,0:T(8,128)(2,1)}, u32[]{:S(2)}, u32[]{:S(2)}) %collective-permute-start.2) | collective-permute-done | bytes 1572896 | tf_op jit(solution)/shard_map/ppermute | solution.py:12
  76.2 21.2 %collective-permute-done.1 = bf16[1024,768]{1,0:T(8,128)(2,1)} collective-permute-done((bf16[1024,768]{1,0:T(8,128)(2,1)}, bf16[1024,768]{1,0:T(8,128)(2,1)}, u32[]{:S(2)}, u32[]{:S(2)}) %collective-permute-start.1) | collective-permute-done | bytes 1572896 | tf_op jit(solution)/shard_map/ppermute | solution.py:12
  97.4 3.8 %collective-permute-start.4 = (bf16[1024,768]{1,0:T(8,128)(2,1)}, bf16[1024,768]{1,0:T(8,128)(2,1)}, u32[]{:S(2)}, u32[]{:S(2)}) collective-permute-start(bf16[1024,768]{1,0:T(8,128)(2,1)} %collective-permute-done.1), channel_id=1, source_target_pairs={{0,96},{8,104},{16,112},{24,120},{32,0},{40,8},{48,16},{56,24},{64... | collective-permute-start | bytes 4718600 | tf_op jit(solution)/shard_map/ppermute | solution.py:12
  101.3 29.8 %collective-permute-done = bf16[1024,768]{1,0:T(8,128)(2,1)} collective-permute-done((bf16[1024,768]{1,0:T(8,128)(2,1)S(1)}, bf16[1024,768]{1,0:T(8,128)(2,1)}, u32[]{:S(2)}, u32[]{:S(2)}) %collective-permute-start) | collective-permute-done | bytes 1572896 | tf_op jit(solution)/shard_map/ppermute | solution.py:12
  131.0 3.1 fusion.89
  134.2 1.7 copy-done.18
  135.9 4.7 %fusion.58 = f32[768,768]{1,0:T(8,128)} fusion(bf16[1024,768]{1,0:T(8,128)(2,1)} %collective-permute-done.1, f32[1024,768]{1,0:T(8,128)S(1)} %fusion.89), kind=kOutput, calls=%fused_computation.83 | convolution fusion | flops 1215037440 | bytes 7077888 | tf_op jit(solution)/shard_map/dot_general | solution.py:33
  140.6 8.1 %fusion.81 = f32[768,768]{1,0:T(8,128)S(1)} fusion(bf16[1024,768]{1,0:T(8,128)(2,1)} %collective-permute-done, f32[1024,768]{1,0:T(8,128)} %copy-done.18, bf16[1024,768]{1,0:T(8,128)(2,1)} %collective-permute-done.1, bf16[1,3072,768]{2,1,0:T(8,128)(2,1)} %param.15, s32[]{:T(128)S(6)} %select_n.29), kind=kOutput, calls=%fused_computation.106 | convolution fusion | flops 2431647744 | bytes 9830404 | tf_op jit(solution)/shard_map/dot_general | solution.py:33
  148.7 4.0 %fusion.85 = f32[1024,768]{1,0:T(8,128)S(1)} fusion(bf16[1024,768]{1,0:T(8,128)(2,1)} %collective-permute-done.2, bf16[1,768,3072]{2,1,0:T(8,128)(2,1)} %param.14, s32[]{:T(128)S(6)} %select_n.29), kind=kOutput, calls=%fused_computation.108 | convolution fusion | flops 1207959552 | bytes 5898244 | tf_op jit(solution)/shard_map/dot_general | solution.py:65
  152.7 1.7 copy-done.17
  154.4 4.7 %fusion.60 = f32[768,768]{1,0:T(8,128)} fusion(bf16[1024,768]{1,0:T(8,128)(2,1)} %collective-permute-done.5, f32[1024,768]{1,0:T(8,128)S(1)} %fusion.85), kind=kOutput, calls=%fused_computation.85 | convolution fusion | flops 1215037440 | bytes 7077888 | tf_op jit(solution)/shard_map/dot_general | solution.py:33
  159.1 9.9 %fusion.77 = f32[768,768]{1,0:T(8,128)} fusion(bf16[1024,768]{1,0:T(8,128)(2,1)} %collective-permute-done.2, f32[1024,768]{1,0:T(8,128)} %copy-done.17, bf16[1024,768]{1,0:T(8,128)(2,1)} %collective-permute-done.5, bf16[1,3072,768]{2,1,0:T(8,128)(2,1)} %param.15, s32[]{:T(128)S(6)} %select_n.29), kind=kOutput, calls=%fused_computation.104 | convolution fusion | flops 2431647744 | bytes 9830404 | tf_op jit(solution)/shard_map/dot_general | solution.py:33
  169.0 4.8 %fusion.87 = f32[1024,768]{1,0:T(8,128)} fusion(bf16[1024,768]{1,0:T(8,128)(2,1)} %collective-permute-done.3, bf16[1,768,3072]{2,1,0:T(8,128)(2,1)} %param.14, s32[]{:T(128)S(6)} %select_n.29), kind=kOutput, calls=%fused_computation.110 | convolution fusion | flops 1207959552 | bytes 5898244 | tf_op jit(solution)/shard_map/dot_general | solution.py:65
  173.8 9.6 %fusion.79 = f32[768,768]{1,0:T(8,128)} fusion(bf16[1024,768]{1,0:T(8,128)(2,1)} %collective-permute-done.3, f32[1024,768]{1,0:T(8,128)} %fusion.87, bf16[1024,768]{1,0:T(8,128)(2,1)} %collective-permute-done.4, bf16[1,3072,768]{2,1,0:T(8,128)(2,1)} %param.15, s32[]{:T(128)S(6)} %select_n.29), kind=kOutput, calls=%fused_computation.105 | convolution fusion | flops 2431647744 | bytes 9830404 | tf_op jit(solution)/shard_map/dot_general | solution.py:33
  183.3 12.8 %multiply_reduce_fusion.19 = (f32[]{:T(128)}, f32[]{:T(128)}, f32[]{:T(128)}, f32[]{:T(128)}, f32[]{:T(128)}, /*index=5*/f32[]{:T(128)}, f32[]{:T(128)}, f32[]{:...) fusion(f32[768,768]{1,0:T(8,128)} %fusion.77, f32[768,768]{1,0:T(8,128)} %fusion.79, f32[768,768]{1,0:T(8,128)S(1)} %fusion.81, ...), kind=kOutput, calls=%fused_computation.74 | convolution fusion | flops 2443444224 | bytes 16908332 | tf_op jit(solution)/shard_map/dot_general | solution.py:33
  196.1 4.3 %fusion.59 = f32[768,768]{1,0:T(8,128)S(1)} fusion(bf16[1024,768]{1,0:T(8,128)(2,1)} %collective-permute-done.4, f32[1024,768]{1,0:T(8,128)} %fusion.87), kind=kOutput, calls=%fused_computation.84 | convolution fusion | flops 1215037440 | bytes 7077888 | tf_op jit(solution)/shard_map/dot_general | solution.py:33
  200.9 7.3 %multiply_reduce_fusion.18 = (f32[]{:T(128)}, f32[]{:T(128)}, f32[]{:T(128)}, f32[]{:T(128)}, f32[]{:T(128)}, /*index=5*/f32[]{:T(128)}, f32[]{:T(128)}, f32[]{:...) fusion(f32[768,768]{1,0:T(8,128)S(1)} %copy-done.4, f32[768,768]{1,0:T(8,128)S(1)} %fusion.59, ...), kind=kOutput, calls=%fused_computation.73 | convolution fusion | flops 1226833920 | bytes 14155816 | tf_op jit(solution)/shard_map/dot_general | solution.py:33
  221.1 2.5 collective-permute-start.6
  223.6 2.7 collective-permute-done.6
  227.4 4.2 %collective-permute-done.7 = f32[4,4]{1,0:T(4,128)S(1)} collective-permute-done((f32[4,4]{1,0:T(4,128)S(1)}, f32[4,4]{1,0:T(4,128)S(1)}, u32[]{:S(2)}, u32[]{:S(2)}) %collective-permute-start.7) | collective-permute-done | bytes 96 | tf_op jit(solution)/shard_map/ppermute | solution.py:12
  244.7 7.7 %multiply_add_fusion = f32[768,768]{1,0:T(8,128)} fusion(f32[768,768]{1,0:T(8,128)} %fusion.60, f32[768,768]{1,0:T(8,128)} %copy-done.5, f32[768,768]{1,0:T(8,128)S(1)} %copy-done.3, f32[768,768]{1,0:T(8,128)} %get-tuple-element.110, f32[]{:T(128)} %bitcast.46, f32[]{:T(128)} %bitcast.45, f32[]{:T(128)} %bitcast.44, f32[]{:T(128)} %bitcast.43), kind=kLoop, calls=%fused_computation.53 | loop fusion | flops 4128768 | bytes 11796496 | tf_op jit(solution)/shard_map/add | solution.py:160
  252.4 4.5 %all-to-all-start.4 = ((f32[4,192,768]{2,1,0:T(8,128)}), f32[4,192,768]{2,1,0:T(8,128)S(1)}, u32[]{:S(2)}, u32[]{:S(2)}) async-start(f32[4,192,768]{2,1,0:T(8,128)} %bitcast.218), calls=%async_computation.4 | async-start | bytes 4718592 | tf_op jit(solution)/shard_map/all_to_all | solution.py:168
  256.8 8.3 %multiply_add_fusion.1 = f32[768,768]{1,0:T(8,128)} fusion(f32[768,768]{1,0:T(8,128)} %fusion.77, f32[768,768]{1,0:T(8,128)} %fusion.79, f32[768,768]{1,0:T(8,128)} %copy-done.2, f32[768,768]{1,0:T(8,128)} %get-tuple-element.109, f32[]{:T(128)} %bitcast.46, f32[]{:T(128)} %bitcast.45, f32[]{:T(128)} %bitcast.44, f32[]{:T(128)} %bitcast.43), kind=kLoop, calls=%fused_computation.54 | loop fusion | flops 4128768 | bytes 11796496 | tf_op jit(solution)/shard_map/add | solution.py:159
  265.2 16.2 %all-to-all-done.4 = f32[4,192,768]{2,1,0:T(8,128)S(1)} async-done(((f32[4,192,768]{2,1,0:T(8,128)}), f32[4,192,768]{2,1,0:T(8,128)S(1)}, u32[]{:S(2)}, u32[]{:S(2)}) %all-to-all-start.4) | async-done | bytes 2359328 | tf_op jit(solution)/shard_map/all_to_all | solution.py:168
  281.4 4.5 %all-to-all-start.3 = ((f32[16,48,768]{2,1,0:T(8,128)}), f32[16,48,768]{2,1,0:T(8,128)}, u32[]{:S(2)}, u32[]{:S(2)}) async-start(f32[16,48,768]{2,1,0:T(8,128)} %bitcast.217), calls=%async_computation.3 | async-start | bytes 4718592 | tf_op jit(solution)/shard_map/all_to_all | solution.py:164
  285.8 15.6 %fusion.50 = bf16[1024,768]{1,0:T(8,128)(2,1)} fusion(bf16[1,3072,768]{2,1,0:T(8,128)(2,1)} %param.15, bf16[1024,768]{1,0:T(8,128)(2,1)} %bitcast.223, bf16[1,768,3072]{2,1,0:T(8,128)(2,1)} %param.14), kind=kOutput, calls=%fused_computation.81 | convolution fusion | flops 9692774400 | bytes 12582912 | tf_op jit(solution)/shard_map/dot_general | solution.py:133
  302.6 11.8 %all-to-all-done.3 = f32[16,48,768]{2,1,0:T(8,128)} async-done(((f32[16,48,768]{2,1,0:T(8,128)}), f32[16,48,768]{2,1,0:T(8,128)}, u32[]{:S(2)}, u32[]{:S(2)}) %all-to-all-start.3) | async-done | bytes 2359328 | tf_op jit(solution)/shard_map/all_to_all | solution.py:164
  314.4 4.3 %all-to-all-start.1 = ((bf16[8,128,768]{2,1,0:T(8,128)(2,1)}), bf16[8,128,768]{2,1,0:T(8,128)(2,1)}, u32[]{:S(2)}, u32[]{:S(2)}) async-start(bf16[8,128,768]{2,1,0:T(8,128)(2,1)} %bitcast.224), calls=%async_computation.1 | async-start | bytes 3145728 | tf_op jit(solution)/shard_map/all_to_all | solution.py:137
  318.7 2.5 slice_bitcast_fusion.29
  321.2 3.3 slice_bitcast_fusion.31
  328.0 2.2 multiply_reduce_fusion.39
  333.9 2.0 multiply_reduce_fusion.29
  344.8 3.1 collective-permute-done.8
  348.0 5.1 %collective-permute-done.9 = f32[4,4]{1,0:T(4,128)S(1)} collective-permute-done((f32[4,4]{1,0:T(4,128)S(1)}, f32[4,4]{1,0:T(4,128)S(1)}, u32[]{:S(2)}, u32[]{:S(2)}) %collective-permute-start.9) | collective-permute-done | bytes 96 | tf_op jit(solution)/shard_map/ppermute | solution.py:182
  353.3 3.5 collective-permute-done.10
  357.9 3.6 multiply_convert_fusion.9
  374.2 3.6 multiply_subtract_fusion.1
  377.8 2.9 multiply_subtract_fusion
  (80 shorter events, 14.8 us)
Async XLA Ops:
  0.6 3.6 copy-start
  4.3 6.6 %copy-start.14 = (bf16[512,768]{1,0:T(8,128)(2,1)S(1)}, bf16[512,768]{1,0:T(8,128)(2,1)}, u32[]{:S(2)}) copy-start(bf16[512,768]{1,0:T(8,128)(2,1)} %param.13) | copy-start | bytes 2359300
  4.3 6.6 %copy-start.15 = (f32[512,1]{0,1:T(1,128)S(1)}, f32[512,1]{0,1:T(1,128)}, u32[]{:S(2)}) copy-start(f32[512,1]{0,1:T(1,128)} %param.12) | copy-start | bytes 6148
  6.5 26.0 %all-to-all-start = ((bf16[8,128,768]{2,1,0:T(8,128)(2,1)}), bf16[8,128,768]{2,1,0:T(8,128)(2,1)S(1)}, u32[]{:S(2)}, u32[]{:S(2)}) async-start(bf16[8,128,768]{2,1,0:T(8,128)(2,1)} %bitcast.5), calls=%async_computation | async-start | bytes 3145728 | tf_op jit(solution)/shard_map/all_to_all | solution.py:111
  32.4 36.3 %copy-start.7 = (bf16[8,128,768]{2,1,0:T(8,128)(2,1)}, bf16[8,128,768]{2,1,0:T(8,128)(2,1)S(1)}, u32[]{:S(2)}) copy-start(bf16[8,128,768]{2,1,0:T(8,128)(2,1)S(1)} %all-to-all-done) | copy-start | bytes 4718596
  32.4 25.9 %all-to-all-start.2 = ((bf16[8,128,768]{2,1,0:T(8,128)(2,1)}), bf16[8,128,768]{2,1,0:T(8,128)(2,1)}, u32[]{:S(2)}, u32[]{:S(2)}) async-start(bf16[8,128,768]{2,1,0:T(8,128)(2,1)} %bitcast.11), calls=%async_computation.2 | async-start | bytes 3145728 | tf_op jit(solution)/shard_map/all_to_all | solution.py:111
  36.7 39.5 %collective-permute-start.2 = (bf16[1024,768]{1,0:T(8,128)(2,1)S(1)}, bf16[1024,768]{1,0:T(8,128)(2,1)}, u32[]{:S(2)}, u32[]{:S(2)}) collective-permute-start(bf16[1024,768]{1,0:T(8,128)(2,1)S(1)} %bitcast.219), channel_id=1, source_target_pairs={{0,32},{8,40},{16,48},{24,56},{32,64},{40,72},{48,80},{56,88},{64,... | collective-permute-start | bytes 4718600 | tf_op jit(solution)/shard_map/ppermute | solution.py:12
  58.3 39.1 %collective-permute-start.1 = (bf16[1024,768]{1,0:T(8,128)(2,1)}, bf16[1024,768]{1,0:T(8,128)(2,1)}, u32[]{:S(2)}, u32[]{:S(2)}) collective-permute-start(bf16[1024,768]{1,0:T(8,128)(2,1)} %bitcast.12), channel_id=1, source_target_pairs={{0,96},{8,104},{16,112},{24,120},{32,0},{40,8},{48,16},{56,24},{64... | collective-permute-start | bytes 4718600 | tf_op jit(solution)/shard_map/ppermute | solution.py:12
  62.3 68.7 %collective-permute-start = (bf16[1024,768]{1,0:T(8,128)(2,1)S(1)}, bf16[1024,768]{1,0:T(8,128)(2,1)}, u32[]{:S(2)}, u32[]{:S(2)}) collective-permute-start(bf16[1024,768]{1,0:T(8,128)(2,1)S(1)} %bitcast.220), channel_id=1, source_target_pairs={{0,96},{8,104},{16,112},{24,120},{32,0},{40,8},{48,16},{56,24},{64... | collective-permute-start | bytes 4718600 | tf_op jit(solution)/shard_map/ppermute | solution.py:12
  62.7 89.9 %collective-permute-start.5 = (bf16[1024,768]{1,0:T(8,128)(2,1)}, bf16[1024,768]{1,0:T(8,128)(2,1)}, u32[]{:S(2)}, u32[]{:S(2)}) collective-permute-start(bf16[1024,768]{1,0:T(8,128)(2,1)} %bitcast.12), channel_id=1, source_target_pairs={{0,32},{8,40},{16,48},{24,56},{32,64},{40,72},{48,80},{56,88},{64,... | collective-permute-start | bytes 4718600 | tf_op jit(solution)/shard_map/ppermute | solution.py:12
  76.2 92.8 %collective-permute-start.3 = (bf16[1024,768]{1,0:T(8,128)(2,1)}, bf16[1024,768]{1,0:T(8,128)(2,1)}, u32[]{:S(2)}, u32[]{:S(2)}) collective-permute-start(bf16[1024,768]{1,0:T(8,128)(2,1)} %collective-permute-done.2), channel_id=1, source_target_pairs={{0,32},{8,40},{16,48},{24,56},{32,64},{40,72},{48,80},{56,88},{64,... | collective-permute-start | bytes 4718600 | tf_op jit(solution)/shard_map/ppermute | solution.py:12
  97.4 76.3 %collective-permute-start.4 = (bf16[1024,768]{1,0:T(8,128)(2,1)}, bf16[1024,768]{1,0:T(8,128)(2,1)}, u32[]{:S(2)}, u32[]{:S(2)}) collective-permute-start(bf16[1024,768]{1,0:T(8,128)(2,1)} %collective-permute-done.1), channel_id=1, source_target_pairs={{0,96},{8,104},{16,112},{24,120},{32,0},{40,8},{48,16},{56,24},{64... | collective-permute-start | bytes 4718600 | tf_op jit(solution)/shard_map/ppermute | solution.py:12
  134.2 1.7 copy-start.18
  148.7 34.7 %copy-start.2 = (f32[768,768]{1,0:T(8,128)}, f32[768,768]{1,0:T(8,128)S(1)}, u32[]{:S(2)}) copy-start(f32[768,768]{1,0:T(8,128)S(1)} %fusion.81) | copy-start | bytes 7077892
  152.7 1.7 copy-start.17
  196.1 4.3 %copy-start.3 = (f32[768,768]{1,0:T(8,128)S(1)}, f32[768,768]{1,0:T(8,128)}, u32[]{:S(2)}) copy-start(f32[768,768]{1,0:T(8,128)} %fusion.58) | copy-start | bytes 7077892
  196.1 4.4 %copy-start.4 = (f32[768,768]{1,0:T(8,128)S(1)}, f32[768,768]{1,0:T(8,128)}, u32[]{:S(2)}) copy-start(f32[768,768]{1,0:T(8,128)} %fusion.60) | copy-start | bytes 7077892
  196.1 4.7 %copy-start.16 = (f32[1024,768]{1,0:T(8,128)S(1)}, f32[1024,768]{1,0:T(8,128)}, u32[]{:S(2)}) copy-start(f32[1024,768]{1,0:T(8,128)} %fusion.91) | copy-start | bytes 9437188
  200.9 7.3 %copy-start.5 = (f32[768,768]{1,0:T(8,128)}, f32[768,768]{1,0:T(8,128)S(1)}, u32[]{:S(2)}) copy-start(f32[768,768]{1,0:T(8,128)S(1)} %fusion.59) | copy-start | bytes 7077892
  221.1 5.2 %collective-permute-start.6 = (f32[4,4]{1,0:T(4,128)S(1)}, f32[4,4]{1,0:T(4,128)S(1)}, u32[]{:S(2)}, u32[]{:S(2)}) collective-permute-start(f32[4,4]{1,0:T(4,128)S(1)} %multiply_reduce_fusion.40), channel_id=1, source_target_pairs={{0,64},{8,72},{16,80},{24,88},{32,96},{40,104},{48,112},{56,120},{... | collective-permute-start | bytes 200 | tf_op jit(solution)/shard_map/ppermute | solution.py:12
  226.3 5.4 %collective-permute-start.7 = (f32[4,4]{1,0:T(4,128)S(1)}, f32[4,4]{1,0:T(4,128)S(1)}, u32[]{:S(2)}, u32[]{:S(2)}) collective-permute-start(f32[4,4]{1,0:T(4,128)S(1)} %add.375), channel_id=1, source_target_pairs={{0,32},{8,40},{16,48},{24,56},{32,64},{40,72},{48,80},{56,88},{64,... | collective-permute-start | bytes 200 | tf_op jit(solution)/shard_map/ppermute | solution.py:12
  252.4 29.0 %all-to-all-start.4 = ((f32[4,192,768]{2,1,0:T(8,128)}), f32[4,192,768]{2,1,0:T(8,128)S(1)}, u32[]{:S(2)}, u32[]{:S(2)}) async-start(f32[4,192,768]{2,1,0:T(8,128)} %bitcast.218), calls=%async_computation.4 | async-start | bytes 4718592 | tf_op jit(solution)/shard_map/all_to_all | solution.py:168
  281.4 33.0 %all-to-all-start.3 = ((f32[16,48,768]{2,1,0:T(8,128)}), f32[16,48,768]{2,1,0:T(8,128)}, u32[]{:S(2)}, u32[]{:S(2)}) async-start(f32[16,48,768]{2,1,0:T(8,128)} %bitcast.217), calls=%async_computation.3 | async-start | bytes 4718592 | tf_op jit(solution)/shard_map/all_to_all | solution.py:164
  314.4 43.5 %all-to-all-start.1 = ((bf16[8,128,768]{2,1,0:T(8,128)(2,1)}), bf16[8,128,768]{2,1,0:T(8,128)(2,1)}, u32[]{:S(2)}, u32[]{:S(2)}) async-start(bf16[8,128,768]{2,1,0:T(8,128)(2,1)} %bitcast.224), calls=%async_computation.1 | async-start | bytes 3145728 | tf_op jit(solution)/shard_map/all_to_all | solution.py:137
  321.2 4.3 %copy-start.6 = (f32[48,768]{1,0:T(8,128)}, f32[48,768]{1,0:T(8,128)S(1)}, u32[]{:S(2)}) copy-start(f32[48,768]{1,0:T(8,128)S(1)} %get-tuple-element.78) | copy-start | bytes 442372
  321.2 4.3 %copy-start.9 = (f32[48,768]{1,0:T(8,128)}, f32[48,768]{1,0:T(8,128)S(1)}, u32[]{:S(2)}) copy-start(f32[48,768]{1,0:T(8,128)S(1)} %get-tuple-element.72) | copy-start | bytes 442372
  321.2 4.3 %copy-start.10 = (f32[48,768]{1,0:T(8,128)}, f32[48,768]{1,0:T(8,128)S(1)}, u32[]{:S(2)}) copy-start(f32[48,768]{1,0:T(8,128)S(1)} %get-tuple-element.83) | copy-start | bytes 442372
  321.2 4.3 %copy-start.11 = (f32[48,768]{1,0:T(8,128)}, f32[48,768]{1,0:T(8,128)S(1)}, u32[]{:S(2)}) copy-start(f32[48,768]{1,0:T(8,128)S(1)} %get-tuple-element.84) | copy-start | bytes 442372
  324.5 1.0 copy-start.8
  344.2 3.7 collective-permute-start.8
  347.9 5.2 %collective-permute-start.9 = (f32[4,4]{1,0:T(4,128)S(1)}, f32[4,4]{1,0:T(4,128)S(1)}, u32[]{:S(2)}, u32[]{:S(2)}) collective-permute-start(f32[4,4]{1,0:T(4,128)S(1)} %fusion.199), channel_id=1, source_target_pairs={{0,16},{8,24},{16,0},{24,8},{32,48},{40,56},{48,32},{56,40},{64,80... | collective-permute-start | bytes 200 | tf_op jit(solution)/shard_map/ppermute | solution.py:182
  353.1 3.7 collective-permute-start.10
  356.8 5.3 %collective-permute-start.11 = (f32[4,4]{1,0:T(4,128)S(1)}, f32[4,4]{1,0:T(4,128)S(1)}, u32[]{:S(2)}, u32[]{:S(2)}) collective-permute-start(f32[4,4]{1,0:T(4,128)S(1)} %add.408), channel_id=1, source_target_pairs={{0,64},{8,72},{16,80},{24,88},{32,96},{40,104},{48,112},{56,120},{... | collective-permute-start | bytes 200 | tf_op jit(solution)/shard_map/ppermute | solution.py:182
  357.9 16.2 %copy-start.12 = (f32[1,48,768]{2,1,0:T(8,128)S(1)}, f32[1,48,768]{2,1,0:T(8,128)}, u32[]{:S(2)}) copy-start(f32[1,48,768]{2,1,0:T(8,128)} %get-tuple-element.54) | copy-start | bytes 442372
  357.9 16.2 %copy-start.13 = (f32[1,48,768]{2,1,0:T(8,128)S(1)}, f32[1,48,768]{2,1,0:T(8,128)}, u32[]{:S(2)}) copy-start(f32[1,48,768]{2,1,0:T(8,128)} %get-tuple-element.55) | copy-start | bytes 442372
  374.1 6.5 %copy-start.1 = (bf16[512,768]{1,0:T(8,128)(2,1)S(1)}, bf16[512,768]{1,0:T(8,128)(2,1)}, u32[]{:S(2)}) copy-start(bf16[512,768]{1,0:T(8,128)(2,1)} %param.10) | copy-start | bytes 2359300

commit v2 on v0

v2 whole, which is shorter than its diff:
```python
import jax
import jax.numpy as jnp
from jax import lax
from jax.experimental import pallas as pl
from jax.experimental.pallas import tpu as pltpu
from jax.sharding import PartitionSpec as P

eps_adasum = 1e-06
SIDE = 4
LANES = 128
MESH = pl.DeviceIdType.MESH
PAIRS = [(a, b) for a in range(SIDE) for b in range(a, SIDE)]
SLOT = {pair: k for k, pair in enumerate(PAIRS)}


def adam_update(grad, weight, moment, second):
    new_moment = 0.9 * moment + 0.1 * grad
    new_second = 0.999 * second + 0.001 * grad * grad
    corr_one = 1.0 - 0.9**10.0
    corr_two = 1.0 - 0.999**10.0
    update = new_moment / corr_one / (jnp.sqrt(new_second / corr_two) + 1e-08)
    return (weight - 0.001 * update, new_moment, new_second)


def contract_rows(left, right):
    return lax.dot_general(
        left, right, (((0,), (0,)), ((), ())), preferred_element_type=jnp.float32
    )


def dot_nt(left, right):
    return lax.dot_general(
        left, right, (((1,), (1,)), ((), ())), preferred_element_type=jnp.float32
    )


def pair_coefs(ab, aa, bb):
    return 1.0 - ab / (2.0 * (aa + eps_adasum)), 1.0 - ab / (2.0 * (bb + eps_adasum))


def tree_weights(g):
    w0, w2 = pair_coefs(g(0, 2), g(0, 0), g(2, 2))
    w1, w3 = pair_coefs(g(1, 3), g(1, 1), g(3, 3))
    aa = w0 * w0 * g(0, 0) + 2.0 * w0 * w2 * g(0, 2) + w2 * w2 * g(2, 2)
    bb = w1 * w1 * g(1, 1) + 2.0 * w1 * w3 * g(1, 3) + w3 * w3 * g(3, 3)
    ab = w0 * (w1 * g(0, 1) + w3 * g(0, 3)) + w2 * (w1 * g(1, 2) + w3 * g(2, 3))
    u, v = pair_coefs(ab, aa, bb)
    return [u * w0, v * w1, u * w2, v * w3]


def gelu_parts(v):
    root = 0.7978845608028654
    square = v * v
    t = jnp.tanh(root * (v + 0.044715 * (square * v)))
    cdf = 0.5 * (1.0 + t)
    slope = cdf + v * (0.5 * (1.0 - t * t)) * (root * (1.0 + 0.134145 * square))
    return v * cdf, slope


def gelu_only(v):
    root = 0.7978845608028654
    return v * (0.5 * (1.0 + jnp.tanh(root * (v + 0.044715 * (v * v * v)))))


def gram_sums(refs, rows):
    width = refs[0].shape[2]

    def step(i, sums):
        sums = list(sums)
        at = pl.ds(pl.multiple_of(i * 8, 8), 8)
        for ref in refs:
            for c in range(width // LANES):
                cols = slice(c * LANES, (c + 1) * LANES)
                v = [ref[k, at, cols] for k in range(SIDE)]
                for p, (a, b) in enumerate(PAIRS):
                    sums[p] = sums[p] + v[a] * v[b]
        return tuple(sums)

    zero = jnp.zeros((8, LANES), jnp.float32)
    return lax.fori_loop(0, rows // 8, step, (zero,) * len(PAIRS))


def kernel(
    sent_t,
    sent_u,
    w1t,
    win_hbm,
    wout_hbm,
    ret,
    seg_in,
    seg_out,
    tok,
    ups,
    win,
    wout,
    g_in,
    g_out,
    ht,
    hgt,
    eout,
    acc,
    s_in,
    s_out,
    r_in,
    r_out,
    gz_out,
    gz_got,
    gy_out,
    gy_got,
    w_sem,
    loc_sem,
    d_send,
    d_recv,
    zf_send,
    zf_recv,
    far_send,
    far_recv,
    e_send,
    e_recv,
    gz_send,
    gz_recv,
    yo_send,
    yo_recv,
    yi_send,
    yi_recv,
    gy_send,
    gy_recv,
):
    f32 = jnp.float32
    bf16 = jnp.bfloat16
    dp = lax.axis_index("dp")
    me = lax.axis_index("expert")
    z, y = lax.div(dp, SIDE), lax.rem(dp, SIDE)
    x, core = lax.div(me, 2), lax.rem(me, 2)
    cap = sent_t.shape[1]
    chunk = 2 * cap
    part = w1t.shape[0]
    own_rows = pl.ds(pl.multiple_of(me * cap, cap), cap)

    def at_zy(i, j):
        return lax.rem(z + i, SIDE) * SIDE + lax.rem(y + j, SIDE)

    def to(dp_index, expert_index):
        return {"device_id": (dp_index, expert_index), "device_id_type": MESH}

    load_win = pltpu.make_async_copy(win_hbm, win, w_sem.at[0])
    load_wout = pltpu.make_async_copy(wout_hbm, wout, w_sem.at[1])
    load_wout.start()
    load_win.start()
    own_t = pltpu.make_async_copy(sent_t.at[me], tok.at[0, own_rows], loc_sem.at[0])
    own_u = pltpu.make_async_copy(sent_u.at[me], ups.at[0, own_rows], loc_sem.at[1])
    own_t.start()
    own_u.start()

    barrier = pltpu.get_barrier_semaphore()
    for k in range(1, 8):
        pl.semaphore_signal(barrier, inc=1, **to(dp, lax.rem(me + k, 8)))
    for i in range(SIDE):
        for j in range(SIDE):
            if i or j:
                pl.semaphore_signal(barrier, inc=1, **to(at_zy(i, j), me))
    pl.semaphore_wait(barrier, 7 + SIDE * SIDE - 1)

    dispatch = []
    for q in range(SIDE):
        for c in range(2):
            if q == 0 and c == 0:
                continue
            there = lax.rem(x + (q ^ (q >> 1)), SIDE) * 2 + lax.rem(core + c, 2)
            n = 2 * q + c
            for h, (src, dst) in enumerate(((sent_t, tok), (sent_u, ups))):
                copy = pltpu.make_async_remote_copy(
                    src_ref=src.at[there],
                    dst_ref=dst.at[0, own_rows],
                    send_sem=d_send.at[h, n],
                    recv_sem=d_recv.at[h, n],
                    **to(dp, there),
                )
                copy.start()
                dispatch.append(copy)

    def clear(i, carry):
        at = pl.ds(pl.multiple_of(i * 16, 16), 16)
        for k in range(SIDE):
            g_in[k, at, :] = jnp.zeros((16, g_in.shape[2]), f32)
            g_out[k, at, :] = jnp.zeros((16, g_out.shape[2]), f32)
        return carry

    lax.fori_loop(0, part // 16, clear, 0)
    load_wout.wait()
    w2_rows = pl.ds(pl.multiple_of(z * part, part), part)

    def chip_rows(q):
        return pl.ds(pl.multiple_of(lax.rem(x + SIDE - (q ^ (q >> 1)), SIDE) * chunk, chunk), chunk)

    def grads(slot, rows):
        t = tok[slot, rows, :]
        u = ups[slot, rows, :]
        act, slope = gelu_parts(dot_nt(w1t[...], t))
        ht[...] = act.astype(bf16)
        hgt[...] = (slope * dot_nt(wout[w2_rows, :], u)).astype(bf16)
        g_out[slot] = g_out[slot] + jnp.dot(ht[...], u, preferred_element_type=f32)
        g_in[slot] = g_in[slot] + jnp.dot(hgt[...], t, preferred_element_type=f32)

    def along_z(buf, slot, to_slot, rows, step, send, recv):
        return pltpu.make_async_remote_copy(
            src_ref=buf.at[slot, rows],
            dst_ref=buf.at[to_slot, rows],
            send_sem=send,
            recv_sem=recv,
            **to(at_zy(step, 0), me),
        )

    def first_hop(q):
        rows = chip_rows(q)
        copies = []
        for h, buf in enumerate((tok, ups)):
            copies.append(along_z(buf, 0, 3, rows, 1, zf_send.at[0, h, q], zf_recv.at[0, h, q]))
            copies.append(along_z(buf, 0, 1, rows, 3, zf_send.at[1, h, q], zf_recv.at[1, h, q]))
        return copies

    def second_hop(q):
        rows = chip_rows(q)
        return [
            along_z(tok, 3, 2, rows, 1, far_send.at[0, q], far_recv.at[0, q]),
            along_z(ups, 1, 2, rows, 3, far_send.at[1, q], far_recv.at[1, q]),
        ]

    own_t.wait()
    own_u.wait()
    for h in range(2):
        dispatch[h].wait_recv()
    for copy in first_hop(0):
        copy.start()
    grads(0, chip_rows(0))

    def own_step(q, carry):
        for c in range(2):
            for h, (src, dst) in enumerate(((sent_t, tok), (sent_u, ups))):
                pltpu.make_async_remote_copy(
                    src_ref=src.at[0],
                    dst_ref=dst.at[0, own_rows],
                    send_sem=d_send.at[h, 2 * q + c],
                    recv_sem=d_recv.at[h, 2 * q + c],
                    **to(dp, lax.rem(me + 1, 8)),
                ).wait_recv()
        for copy in first_hop(q):
            copy.start()
        grads(0, chip_rows(q))
        return carry

    lax.fori_loop(1, SIDE, own_step, 0)

    load_win.wait()
    tile = 512
    rows_all = tok.shape[1]
    half = rows_all // 2

    def forward(n, carry):
        cols = pl.ds(pl.multiple_of(n * tile, tile), tile)
        for r in range(2):
            rows = slice(r * half, (r + 1) * half)
            pre = jnp.dot(tok[0, rows, :], win[:, cols], preferred_element_type=f32)
            hid = gelu_only(pre).astype(bf16)
            more = jnp.dot(hid, wout[cols, :], preferred_element_type=f32)
            acc[rows, :] = acc[rows, :] + more
        return carry

    acc[...] = jnp.zeros_like(acc)
    lax.fori_loop(0, win.shape[1] // tile, forward, 0)

    def round_out(i, carry):
        at = pl.ds(pl.multiple_of(i * cap, cap), cap)
        eout[at, :] = acc[at, :].astype(bf16)
        return carry

    lax.fori_loop(0, rows_all // cap, round_out, 0)
    back = []
    for k in range(1, 8):
        there = lax.rem(me + k, 8)
        copy = pltpu.make_async_remote_copy(
            src_ref=eout.at[pl.ds(pl.multiple_of(there * cap, cap), cap)],
            dst_ref=ret.at[me],
            send_sem=e_send.at[k],
            recv_sem=e_recv.at[k],
            **to(dp, there),
        )
        copy.start()
        back.append(copy)
    back_own = pltpu.make_async_copy(eout.at[own_rows], ret.at[me], loc_sem.at[2])
    back_own.start()

    def near_step(q, carry):
        for copy in first_hop(q):
            copy.wait_recv()
        for copy in second_hop(q):
            copy.start()
        grads(1, chip_rows(q))
        grads(3, chip_rows(q))
        return carry

    lax.fori_loop(0, SIDE, near_step, 0)

    def far_step(q, carry):
        for copy in second_hop(q):
            copy.wait_recv()
        grads(2, chip_rows(q))
        return carry

    lax.fori_loop(0, SIDE, far_step, 0)

    for p, s in enumerate(gram_sums((g_in, g_out), part)):
        gz_out[p : p + 1, :] = jnp.sum(s, axis=0, keepdims=True)
    sums_z = []
    for i in range(1, SIDE):
        copy = pltpu.make_async_remote_copy(
            src_ref=gz_out,
            dst_ref=gz_got.at[SIDE - i],
            send_sem=gz_send.at[SIDE - i],
            recv_sem=gz_recv.at[SIDE - i],
            **to(at_zy(i, 0), me),
        )
        copy.start()
        sums_z.append(copy)
    total = [gz_out[p : p + 1, :] for p in range(len(PAIRS))]
    for copy in sums_z:
        copy.wait_recv()
    for i in range(1, SIDE):
        for p, (a, b) in enumerate(PAIRS):
            q = SLOT[tuple(sorted(((a + i) % SIDE, (b + i) % SIDE)))]
            total[q] = total[q] + gz_got[i, p : p + 1, :]
    total = [jnp.sum(t, axis=1, keepdims=True) for t in total]
    w = tree_weights(lambda a, b: total[SLOT[(a, b)]])

    rows_out = seg_out.shape[0]
    rows_in = seg_in.shape[0]
    sends = []
    for j in (1, 3, 2, 0):
        there = lax.rem(y + j, SIDE)
        base = there * rows_out

        def mix_out(n, carry, j=j, base=base):
            at = pl.ds(pl.multiple_of(base + n * 16, 16), 16)
            v = w[0] * g_out[0, at, :] + w[1] * g_out[1, at, :]
            v = v + w[2] * g_out[2, at, :] + w[3] * g_out[3, at, :]
            if j:
                s_out[at, :] = v
            else:
                r_out[0, pl.ds(pl.multiple_of(n * 16, 16), 16), :] = v
            return carry

        lax.fori_loop(0, rows_out // 16, mix_out, 0)
        if j:
            copy = pltpu.make_async_remote_copy(
                src_ref=s_out.at[pl.ds(pl.multiple_of(base, 8), rows_out)],
                dst_ref=r_out.at[SIDE - j],
                send_sem=yo_send.at[SIDE - j],
                recv_sem=yo_recv.at[SIDE - j],
                **to(at_zy(0, j), me),
            )
            copy.start()
            sends.append(copy)

    def mix_in(n, carry):
        cols = pl.ds(pl.multiple_of(n * LANES, LANES), LANES)
        for m in range(part // LANES):
            at = slice(m * LANES, (m + 1) * LANES)
            v = w[0] * g_in[0, at, cols] + w[1] * g_in[1, at, cols]
            v = v + w[2] * g_in[2, at, cols] + w[3] * g_in[3, at, cols]
            s_in[cols, at] = v.T
        return carry

    lax.fori_loop(0, s_in.shape[0] // LANES, mix_in, 0)
    own_block = pl.ds(pl.multiple_of(z * rows_in, 8), rows_in)
    for j in (1, 3, 2, 0):
        for i in range(SIDE):
            block = at_zy(i, j)
            src = s_in.at[pl.ds(pl.multiple_of(block * rows_in, 8), rows_in)]
            if i or j:
                k = (SIDE - i) % SIDE * SIDE + (SIDE - j) % SIDE
                copy = pltpu.make_async_remote_copy(
                    src_ref=src,
                    dst_ref=r_in.at[(SIDE - j) % SIDE, own_block],
                    send_sem=yi_send.at[k],
                    recv_sem=yi_recv.at[k],
                    **to(block, me),
                )
                copy.start()
                sends.append(copy)
            else:
                keep = pltpu.make_async_copy(src, r_in.at[0, own_block], loc_sem.at[3])
                keep.start()
    for copy in sends:
        copy.wait_recv()
    keep.wait()

    for p, s in enumerate(gram_sums((r_in, r_out), rows_out)):
        gy_out[p : p + 1, :] = jnp.sum(s, axis=0, keepdims=True)
    sums_y = []
    for i in range(SIDE):
        for j in range(SIDE):
            if i or j:
                k = (SIDE - i) % SIDE * SIDE + (SIDE - j) % SIDE
                copy = pltpu.make_async_remote_copy(
                    src_ref=gy_out,
                    dst_ref=gy_got.at[k],
                    send_sem=gy_send.at[k],
                    recv_sem=gy_recv.at[k],
                    **to(at_zy(i, j), me),
                )
                copy.start()
                sums_y.append(copy)
    total = [gy_out[p : p + 1, :] for p in range(len(PAIRS))]
    for copy in sums_y:
        copy.wait_recv()
    for j in range(SIDE):
        for i in range(SIDE):
            if i or j:
                for p, (a, b) in enumerate(PAIRS):
                    q = SLOT[tuple(sorted(((a + j) % SIDE, (b + j) % SIDE)))]
                    total[q] = total[q] + gy_got[i * SIDE + j, p : p + 1, :]
    total = [jnp.sum(t, axis=1, keepdims=True) for t in total]
    v = tree_weights(lambda a, b: total[SLOT[(a, b)]])
    for i in range(SIDE):
        at = slice(i * rows_in, (i + 1) * rows_in)
        seg_in[:, i * part : (i + 1) * part] = (
            v[0] * r_in[0, at, :] + v[1] * r_in[1, at, :]
        ) + (v[2] * r_in[2, at, :] + v[3] * r_in[3, at, :])
        at = slice(i * rows_in, (i + 1) * rows_in)
        seg_out[at, :] = (v[0] * r_out[0, at, :] + v[1] * r_out[1, at, :]) + (
            v[2] * r_out[2, at, :] + v[3] * r_out[3, at, :]
        )

    for copy in dispatch:
        copy.wait_send()

    def drain(q, carry):
        for copy in first_hop(q) + second_hop(q):
            copy.wait_send()
        return carry

    lax.fori_loop(0, SIDE, drain, 0)
    for copy in back:
        copy.wait()
    back_own.wait()
    for copy in sums_z + sends + sums_y:
        copy.wait_send()


def expert_step(sent_t, sent_u, w1t, w_in, w_out):
    f32 = jnp.float32
    bf16 = jnp.bfloat16
    experts, cap, width = sent_t.shape
    rows = experts * cap
    part = w1t.shape[0]
    side = SIDE
    any_space = pl.BlockSpec(memory_space=pl.ANY)
    vmem = pl.BlockSpec(memory_space=pltpu.VMEM)
    rows_in = width // (side * side)
    rows_out = part // side
    dma = pltpu.SemaphoreType.DMA
    return pl.pallas_call(
        kernel,
        out_shape=(
            jax.ShapeDtypeStruct((experts, cap, width), bf16),
            jax.ShapeDtypeStruct((rows_in, side * part), f32),
            jax.ShapeDtypeStruct((rows_out, width), f32),
        ),
        in_specs=[any_space, any_space, vmem, any_space, any_space],
        out_specs=(any_space, vmem, vmem),
        scratch_shapes=[
            pltpu.VMEM((side, rows, width), bf16),
            pltpu.VMEM((side, rows, width), bf16),
            pltpu.VMEM(w_in.shape, bf16),
            pltpu.VMEM(w_out.shape, bf16),
            pltpu.VMEM((side, part, width), f32),
            pltpu.VMEM((side, part, width), f32),
            pltpu.VMEM((part, 2 * cap), bf16),
            pltpu.VMEM((part, 2 * cap), bf16),
            pltpu.VMEM((rows, width), bf16),
            pltpu.VMEM((rows, width), f32),
            pltpu.VMEM((width, part), f32),
            pltpu.VMEM((part, width), f32),
            pltpu.VMEM((side, side * rows_in, part), f32),
            pltpu.VMEM((side, rows_out, width), f32),
            pltpu.VMEM((16, LANES), f32),
            pltpu.VMEM((side, 16, LANES), f32),
            pltpu.VMEM((16, LANES), f32),
            pltpu.VMEM((side * side, 16, LANES), f32),
            dma((2,)),
            dma((4,)),
            dma((2, 8)),
            dma((2, 8)),
            dma((2, 2, side)),
            dma((2, 2, side)),
            dma((2, side)),
            dma((2, side)),
            dma((8,)),
            dma((8,)),
            dma((side,)),
            dma((side,)),
            dma((side,)),
            dma((side,)),
            dma((side * side,)),
            dma((side * side,)),
            dma((side * side,)),
            dma((side * side,)),
        ],
        compiler_params=pltpu.CompilerParams(
            collective_id=0, has_side_effects=True, vmem_limit_bytes=66_000_000
        ),
        name="expert_step",
    )(sent_t, sent_u, w1t, w_in, w_out)


def body(
    tokens,
    assigned,
    gate_prob,
    cotangent,
    weight_in,
    weight_out,
    moment_in,
    moment_out,
    second_in,
    second_out,
):
    f32 = jnp.float32
    bf16 = jnp.bfloat16
    experts = lax.axis_size("expert")
    replicas = lax.axis_size("dp")
    self_index = lax.axis_index("dp")
    z_index = self_index // SIDE
    tok_rows, width = tokens.shape
    hidden_width = weight_in.shape[2]
    part = hidden_width // SIDE
    capacity = 2 * tok_rows // experts
    buffer_rows = experts * capacity
    expert_ids = assigned[:, 0]
    one_hot = (expert_ids[:, None] == jnp.arange(experts, dtype=jnp.int32)[None, :]).astype(
        jnp.int32
    )
    slot_index = jnp.sum((jnp.cumsum(one_hot, axis=0) - one_hot) * one_hot, axis=1)
    slot_code = expert_ids * capacity + slot_index
    table = (jnp.arange(buffer_rows, dtype=jnp.int32)[:, None] == slot_code[None, :]).astype(bf16)
    scaled = (gate_prob * cotangent.astype(f32)).astype(bf16)

    def placed(rows):
        out = jnp.dot(table, rows, preferred_element_type=f32).astype(bf16)
        return out.reshape(experts, capacity, width)

    w_first = weight_in[0]
    w_second = weight_out[0]
    w1t = lax.dynamic_slice_in_dim(w_first, z_index * part, part, 1).T
    returned, seg_first, seg_second = expert_step(
        placed(tokens), placed(scaled), w1t, w_first, w_second
    )
    picked = contract_rows(table, returned.reshape(buffer_rows, width))
    combined = (gate_prob * picked).astype(bf16)

    rows_first = width // replicas
    rows_second = hidden_width // replicas
    own_first = lax.dynamic_slice_in_dim(w_first, self_index * rows_first, rows_first, 0).astype(
        f32
    )
    own_second = lax.dynamic_slice_in_dim(
        w_second, self_index * rows_second, rows_second, 0
    ).astype(f32)
    new_w_first, new_m_first, new_v_first = adam_update(
        seg_first, own_first, moment_in[0], second_in[0]
    )
    new_w_second, new_m_second, new_v_second = adam_update(
        seg_second, own_second, moment_out[0], second_out[0]
    )
    return (
        combined,
        new_w_first[None],
        new_w_second[None],
        new_m_first[None],
        new_m_second[None],
        new_v_first[None],
        new_v_second[None],
    )


def solution(mesh):
    return jax.shard_map(
        body,
        mesh=mesh,
        in_specs=(
            P(("dp", "expert"), None),
            P(("dp", "expert"), None),
            P(("dp", "expert"), None),
            P(("dp", "expert"), None),
            P("expert", None, None),
            P("expert", None, None),
            P("expert", "dp", None),
            P("expert", "dp", None),
            P("expert", "dp", None),
            P("expert", "dp", None),
        ),
        out_specs=(
            P(("dp", "expert"), None),
            P("expert", "dp", None),
            P("expert", "dp", None),
            P("expert", "dp", None),
            P("expert", "dp", None),
            P("expert", "dp", None),
            P("expert", "dp", None),
        ),
        check_vma=False,
    )
```

time: 629 us -> 210 us (0.33)
  waiting for transfers between devices: 401 us -> 0 us
  Pallas kernels: 0 us -> 192 us
  matrix products: 61.5 us -> 6.62 us
  local copies, waits for them, and re-layouts: 53.7 us -> 3.16 us
  other arithmetic: 55.1 us -> 7.22 us
  starting transfers between devices: 44.9 us -> 0 us
  between operations: 11.3 us -> 0.77 us
    ppermute x14 -> x0, waiting for transfers between devices: 371 us -> none  [from_partner(): lax.ppermute(x, axis, [(i, i ^ 1 << bit) for i in range(lax.axis_size(axi...]
    pallas_call x0 -> x1, Pallas kernels: none -> 192 us  [expert_step(): pl.pallas_call(kernel, out_shape=(jax.ShapeDtypeStruct((experts, cap, wid...]
    dot_general x3 -> x1, matrix products: 35.4 us -> 2.11 us  [contract_rows(): lax.dot_general(left, right, (((0,), (0,)), ((), ())), preferred_element_...]
    ppermute x14 -> x0, starting transfers between devices: 31.7 us -> none  [from_partner(): lax.ppermute(x, axis, [(i, i ^ 1 << bit) for i in range(lax.axis_size(axi...]
    all_to_all x3 -> x0, waiting for transfers between devices: 30.3 us -> none  [the longest x1 19.2 us: body(): lax.all_to_all(sent_tokens, 'expert', split_axis=0, concat_axis=0, tiled=...]
    another operation x6 -> x1, local copies, waits for them, and re-layouts: 30.2 us -> 0.01 us  [the longest x3 29.9 us: body(): vectors = jnp.stack([grad_in.reshape(-1, 128), grad_out.reshape(-1, 128)])]
    dot_general x4 -> x2, matrix products: 26 us -> 4.5 us  [placed(): out = jnp.dot(table, rows, preferred_element_type=f32).astype(bf16)]
    add x14 -> x0, other arithmetic: 19.1 us -> none  [the longest x10 14.1 us: group_total(): summed = summed + from_partner(summed, 'dp', other_bit)]
  transfers between devices with their start and end apart: 17 -> 0, of which waited for: 16 -> 0; matrix products, arithmetic and copies ran while one was open for 6% -> 0% of each run, Pallas kernels for 0% -> 0%
where the time goes in v2:
time: 210 us
  Pallas kernels  192 us (91%)
  other arithmetic  7.22 us (3%)
  matrix products  6.62 us (3%)
  local copies, waits for them, and re-layouts  3.16 us (2%)
    pallas_call x1, Pallas kernels, expert_step(): pl.pallas_call(kernel, out_shape=(jax.ShapeDtypeStruct((experts, cap, wid...  192 us
    dot_general x2, matrix products, placed(): out = jnp.dot(table, rows, preferred_element_type=f32).astype(bf16)  4.5 us

profile of v2, /device:TPU:0, one launch (start us, length us, event | category | flops | bytes accessed | tf_op | source)
XLA Modules:
  0.0 210.2 jit_solution(12489708767562995205)
XLA Ops:
  0.6 0.0 copy-start
  0.7 1.4 constant_dynamic-slice_fusion
  2.1 0.0 copy-start.4
  2.1 0.0 copy-start.6
  2.1 0.0 copy-start.7
  2.1 1.5 copy.18
  3.6 0.0 copy-done.4
  3.6 1.1 reduce-window.6
  4.7 0.2 slice_reduce_fusion
  5.0 0.1 fusion.18
  5.1 0.0 copy-done.6
  5.1 0.0 copy-done.7
  5.1 2.3 %fusion.4 = bf16[1024,768]{1,0:T(8,128)(2,1)} fusion(s32[512]{0:T(512)S(1)} %multiply_add_fusion, bf16[512,768]{1,0:T(8,128)(2,1)S(1)} %copy-done.6, f32[512]{0:T(512)S(1)} %bitcast.72), kind=kOutput, calls=%fused_computation.5 | convolution fusion | flops 807796736 | bytes 2363392 | tf_op jit(solution)/shard_map/dot_general | solution.py:549
  7.4 0.0 copy-done
  7.4 2.2 %fusion.3 = bf16[1024,768]{1,0:T(8,128)(2,1)} fusion(bf16[512,768]{1,0:T(8,128)(2,1)S(1)} %copy-done, s32[512]{0:T(512)S(1)} %multiply_add_fusion), kind=kOutput, calls=%fused_computation.4 | convolution fusion | flops 806617088 | bytes 2361344 | tf_op jit(solution)/shard_map/dot_general | solution.py:549
  9.6 192.5 %expert_step.1 = (bf16[8,128,768]{2,1,0:T(8,128)(2,1)}, f32[48,3072]{1,0:T(8,128)}, f32[192,768]{1,0:T(8,128)}) custom-call(bf16[8,128,768]{2,1,0:T(8,128)(2,1)} %bitcast.67, bf16[8,128,768]{2,1,0:T(8,128)(2,1)} %bitcast.66, bf16[768,768]{1,0:T(8,128)(2,1)} %bitcast.65, bf16[768,3072]{1,0:T(8,128)(2,1)} %bitcast.63, bf16[3072,768]{1,0:T(8,128)(2,1)} %bitcast.64), custom_call_target="tpu_custom_call" | custom-call | tf_op jit(solution)/shard_map/expert_step/pallas_call | solution.py:462
  202.1 0.0 copy-start.1
  202.1 0.0 copy-start.2
  202.1 0.0 copy-start.3
  202.1 3.2 %fusion.15 = (f32[1,192,768]{2,1,0:T(8,128)}, f32[1,192,768]{2,1,0:T(8,128)}, f32[1,192,768]{2,1,0:T(8,128)}) fusion(f32[192,768]{1,0:T(8,128)} %get-tuple-element.12, f32[1,192,768]{2,1,0:T(8,128)} %param.19, f32[1,192,768]{2,1,0:T(8,128)} %param.17, bf16[1,3072,768]{2,1,0:T(8,128)(2,1)} %param.15, s32[]{:T(128)S(6)} %select_n.17), kind=kLoop, calls=%fused_computation.24 | loop fusion | flops 2064384 | bytes 3833860 | tf_op jit(solution)/shard_map/broadcast_in_dim | solution.py:582
  205.4 0.0 copy-done.1
  205.4 0.0 copy-done.2
  205.4 0.0 copy-done.3
  205.4 0.0 copy-start.5
  205.4 2.7 %fusion.16 = (f32[1,48,3072]{2,1,0:T(8,128)}, f32[1,48,3072]{2,1,0:T(8,128)}, f32[1,48,3072]{2,1,0:T(8,128)}) fusion(f32[48,3072]{1,0:T(8,128)S(1)} %copy-done.3, f32[1,48,3072]{2,1,0:T(8,128)S(1)} %copy-done.1, f32[1,48,3072]{2,1,0:T(8,128)S(1)} %copy-done.2, bf16[1,768,3072]{2,1,0:T(8,128)(2,1)} %param.14, s32[]{:T(128)S(6)} %select_n.16), kind=kLoop, calls=%fused_computation.25 | loop fusion | flops 2064384 | bytes 3833860 | tf_op jit(solution)/shard_map/broadcast_in_dim | solution.py:581
  208.1 0.0 copy-done.5
  208.1 2.1 %multiply_convert_fusion = bf16[512,768]{1,0:T(8,128)(2,1)} fusion(bf16[1024,768]{1,0:T(8,128)(2,1)S(1)} %bitcast.71, s32[512]{0:T(512)S(1)} %multiply_add_fusion, f32[512]{0:T(512)S(1)} %bitcast.73), kind=kOutput, calls=%fused_computation.6 | convolution fusion | flops 806617088 | bytes 2363392 | tf_op jit(solution)/shard_map/dot_general | solution.py:26
  (4 shorter events, 0.0 us)
Async XLA Ops:
  0.6 6.8 %copy-start = (bf16[512,768]{1,0:T(8,128)(2,1)S(1)}, bf16[512,768]{1,0:T(8,128)(2,1)}, u32[]{:S(2)}) copy-start(bf16[512,768]{1,0:T(8,128)(2,1)} %param.10) | copy-start | bytes 2359300
  2.1 1.5 copy-start.4
  2.1 3.0 %copy-start.6 = (bf16[512,768]{1,0:T(8,128)(2,1)S(1)}, bf16[512,768]{1,0:T(8,128)(2,1)}, u32[]{:S(2)}) copy-start(bf16[512,768]{1,0:T(8,128)(2,1)} %param.13) | copy-start | bytes 2359300
  2.1 3.0 %copy-start.7 = (f32[512,1]{0,1:T(1,128)S(1)}, f32[512,1]{0,1:T(1,128)}, u32[]{:S(2)}) copy-start(f32[512,1]{0,1:T(1,128)} %param.12) | copy-start | bytes 6148
  202.1 3.3 %copy-start.1 = (f32[1,48,3072]{2,1,0:T(8,128)S(1)}, f32[1,48,3072]{2,1,0:T(8,128)}, u32[]{:S(2)}) copy-start(f32[1,48,3072]{2,1,0:T(8,128)} %param.18) | copy-start | bytes 1769476
  202.1 3.3 %copy-start.2 = (f32[1,48,3072]{2,1,0:T(8,128)S(1)}, f32[1,48,3072]{2,1,0:T(8,128)}, u32[]{:S(2)}) copy-start(f32[1,48,3072]{2,1,0:T(8,128)} %param.16) | copy-start | bytes 1769476
  202.1 3.3 %copy-start.3 = (f32[48,3072]{1,0:T(8,128)S(1)}, f32[48,3072]{1,0:T(8,128)}, u32[]{:S(2)}) copy-start(f32[48,3072]{1,0:T(8,128)} %get-tuple-element.11) | copy-start | bytes 1769476
  205.4 2.7 %copy-start.5 = (bf16[8,128,768]{2,1,0:T(8,128)(2,1)S(1)}, bf16[8,128,768]{2,1,0:T(8,128)(2,1)}, u32[]{:S(2)}) copy-start(bf16[8,128,768]{2,1,0:T(8,128)(2,1)} %get-tuple-element.10) | copy-start | bytes 4718596

commit v3 on v2

v3 whole, which is shorter than its diff:
```python
import jax
import jax.numpy as jnp
from jax import lax
from jax.experimental import pallas as pl
from jax.experimental.pallas import tpu as pltpu
from jax.sharding import PartitionSpec as P

eps_adasum = 1e-06
SIDE = 4
LANES = 128
MESH = pl.DeviceIdType.MESH
PAIRS = [(a, b) for a in range(SIDE) for b in range(a, SIDE)]
SLOT = {pair: k for k, pair in enumerate(PAIRS)}


def adam_update(grad, weight, moment, second):
    new_moment = 0.9 * moment + 0.1 * grad
    new_second = 0.999 * second + 0.001 * grad * grad
    corr_one = 1.0 - 0.9**10.0
    corr_two = 1.0 - 0.999**10.0
    update = new_moment / corr_one / (jnp.sqrt(new_second / corr_two) + 1e-08)
    return (weight - 0.001 * update, new_moment, new_second)


def dot_nt(left, right):
    return lax.dot_general(
        left, right, (((1,), (1,)), ((), ())), preferred_element_type=jnp.float32
    )


def pair_coefs(ab, aa, bb):
    return 1.0 - ab / (2.0 * (aa + eps_adasum)), 1.0 - ab / (2.0 * (bb + eps_adasum))


def tree_weights(g):
    w0, w2 = pair_coefs(g(0, 2), g(0, 0), g(2, 2))
    w1, w3 = pair_coefs(g(1, 3), g(1, 1), g(3, 3))
    aa = w0 * w0 * g(0, 0) + 2.0 * w0 * w2 * g(0, 2) + w2 * w2 * g(2, 2)
    bb = w1 * w1 * g(1, 1) + 2.0 * w1 * w3 * g(1, 3) + w3 * w3 * g(3, 3)
    ab = w0 * (w1 * g(0, 1) + w3 * g(0, 3)) + w2 * (w1 * g(1, 2) + w3 * g(2, 3))
    u, v = pair_coefs(ab, aa, bb)
    return [u * w0, v * w1, u * w2, v * w3]


def gelu_parts(v):
    root = 0.7978845608028654
    square = v * v
    t = jnp.tanh(root * (v + 0.044715 * (square * v)))
    cdf = 0.5 * (1.0 + t)
    slope = cdf + v * (0.5 * (1.0 - t * t)) * (root * (1.0 + 0.134145 * square))
    return v * cdf, slope


def gelu_only(v):
    root = 0.7978845608028654
    return v * (0.5 * (1.0 + jnp.tanh(root * (v + 0.044715 * (v * v * v)))))


def columns_of(row):
    return jnp.broadcast_to(row, (LANES, LANES)).T


def encode(v):
    most = jnp.maximum(jnp.max(jnp.abs(v), axis=0, keepdims=True), 1e-30)
    codes = jnp.round(v * (32767.0 / most)).astype(jnp.int32).astype(jnp.int16)
    return codes, most * (1.0 / 32767.0)


def gram_sums(refs, rows):
    width = refs[0].shape[2]

    def step(i, sums):
        sums = list(sums)
        at = pl.ds(pl.multiple_of(i * 8, 8), 8)
        for ref in refs:
            for c in range(width // LANES):
                cols = slice(c * LANES, (c + 1) * LANES)
                v = [ref[k, at, cols] for k in range(SIDE)]
                for p, (a, b) in enumerate(PAIRS):
                    sums[p] = sums[p] + v[a] * v[b]
        return tuple(sums)

    zero = jnp.zeros((8, LANES), jnp.float32)
    return lax.fori_loop(0, rows // 8, step, (zero,) * len(PAIRS))


def kernel(
    assigned,
    gate,
    tokens,
    cotangent,
    win_hbm,
    wout_hbm,
    combined,
    seg_in,
    seg_out,
    tok,
    ups,
    win,
    wout,
    w1t,
    g_in,
    g_out,
    ht,
    hgt,
    sent_t,
    sent_u,
    scaled,
    code_cols,
    gate_cols,
    eout,
    ret,
    pick,
    acc,
    q_in,
    q_out,
    rq_in,
    rq_out,
    f_in,
    f_out,
    rf_in,
    rf_out,
    gz_out,
    gz_got,
    gy_out,
    gy_got,
    w_sem,
    loc_sem,
    d_send,
    d_recv,
    zf_send,
    zf_recv,
    far_send,
    far_recv,
    e_send,
    e_recv,
    gz_send,
    gz_recv,
    yo_send,
    yo_recv,
    yi_send,
    yi_recv,
    gy_send,
    gy_recv,
):
    f32 = jnp.float32
    bf16 = jnp.bfloat16
    dp = lax.axis_index("dp")
    me = lax.axis_index("expert")
    z, y = lax.div(dp, SIDE), lax.rem(dp, SIDE)
    x, core = lax.div(me, 2), lax.rem(me, 2)
    cap = ret.shape[1]
    chunk = 2 * cap
    part = w1t.shape[0]
    toks, width = tokens.shape
    lane_blocks = width // LANES
    own_rows = pl.ds(pl.multiple_of(me * cap, cap), cap)

    def at_zy(i, j):
        return lax.rem(z + i, SIDE) * SIDE + lax.rem(y + j, SIDE)

    def to(dp_index, expert_index):
        return {"device_id": (dp_index, expert_index), "device_id_type": MESH}

    load_win = pltpu.make_async_copy(win_hbm, win, w_sem.at[0])
    load_wout = pltpu.make_async_copy(wout_hbm, wout, w_sem.at[1])
    load_win.start()
    load_wout.start()

    barrier = pltpu.get_barrier_semaphore()
    for k in range(1, 8):
        pl.semaphore_signal(barrier, inc=1, **to(dp, lax.rem(me + k, 8)))
    for i in range(SIDE):
        for j in range(SIDE):
            if i or j:
                pl.semaphore_signal(barrier, inc=1, **to(at_zy(i, j), me))

    named = assigned[...]
    hot = (lax.broadcasted_iota(jnp.int32, (16, toks), 0) == named).astype(f32)
    earlier = (
        lax.broadcasted_iota(jnp.int32, (toks, toks), 0)
        < lax.broadcasted_iota(jnp.int32, (toks, toks), 1)
    ).astype(f32)
    rank = jnp.dot(hot.astype(bf16), earlier.astype(bf16), preferred_element_type=f32)
    place = (named * cap).astype(f32) + jnp.sum(rank * hot, axis=0, keepdims=True)
    for b in range(toks // LANES):
        at = slice(b * LANES, (b + 1) * LANES)
        code_cols[at, :] = columns_of(place[:, at])
        column = columns_of(gate[:, at])
        gate_cols[at, :] = column
        for c in range(lane_blocks):
            cols = slice(c * LANES, (c + 1) * LANES)
            scaled[at, cols] = (column * cotangent[at, cols].astype(f32)).astype(bf16)

    def chip_at(q):
        return lax.rem(x + (q ^ (q >> 1)), SIDE)

    def chip_rows(q):
        return pl.ds(pl.multiple_of(lax.rem(x + SIDE - (q ^ (q >> 1)), SIDE) * chunk, chunk), chunk)

    def place_rows(q):
        base = (chip_at(q) * chunk).astype(f32)
        slots = lax.broadcasted_iota(jnp.int32, (chunk, toks), 0).astype(f32) + base
        table = (slots == place).astype(f32).astype(bf16)
        sent_t[q] = jnp.dot(table, tokens[...], preferred_element_type=f32).astype(bf16)
        sent_u[q] = jnp.dot(table, scaled[...], preferred_element_type=f32).astype(bf16)

    def dispatch(q, c):
        there = lax.rem(core + c, 2)
        return [
            pltpu.make_async_remote_copy(
                src_ref=src.at[q, pl.ds(pl.multiple_of(there * cap, cap), cap)],
                dst_ref=dst.at[0, own_rows],
                send_sem=d_send.at[h, 2 * q + c],
                recv_sem=d_recv.at[h, 2 * q + c],
                **to(dp, chip_at(q) * 2 + there),
            )
            for h, (src, dst) in enumerate(((sent_t, tok), (sent_u, ups)))
        ]

    def along_z(buf, slot, to_slot, rows, step, send, recv):
        return pltpu.make_async_remote_copy(
            src_ref=buf.at[slot, rows],
            dst_ref=buf.at[to_slot, rows],
            send_sem=send,
            recv_sem=recv,
            **to(at_zy(step, 0), me),
        )

    def first_hop(q, c):
        source = lax.rem(x + SIDE - (q ^ (q >> 1)), SIDE) * 2 + lax.rem(core + c, 2)
        rows = pl.ds(pl.multiple_of(source * cap, cap), cap)
        n = 2 * q + c
        copies = []
        for h, buf in enumerate((tok, ups)):
            copies.append(along_z(buf, 0, 3, rows, 1, zf_send.at[0, h, n], zf_recv.at[0, h, n]))
            copies.append(along_z(buf, 0, 1, rows, 3, zf_send.at[1, h, n], zf_recv.at[1, h, n]))
        return copies

    def second_hop(q):
        rows = chip_rows(q)
        return [
            along_z(tok, 3, 2, rows, 1, far_send.at[0, q], far_recv.at[0, q]),
            along_z(ups, 1, 2, rows, 3, far_send.at[1, q], far_recv.at[1, q]),
        ]

    place_rows(0)
    half_rows = pl.ds(pl.multiple_of(core * cap, cap), cap)
    tok[0, own_rows, :] = sent_t[0, half_rows, :]
    ups[0, own_rows, :] = sent_u[0, half_rows, :]
    pl.semaphore_wait(barrier, 7 + SIDE * SIDE - 1)
    for copy in dispatch(0, 1) + first_hop(0, 0):
        copy.start()

    def place_step(q, carry):
        place_rows(q)
        for copy in dispatch(q, 0) + dispatch(q, 1):
            copy.start()
        return carry

    lax.fori_loop(1, SIDE, place_step, 0)
    for copy in dispatch(0, 1):
        copy.wait_recv()
    for copy in first_hop(0, 1):
        copy.start()

    load_win.wait()

    def turn(n, carry):
        at = pl.ds(pl.multiple_of(n * LANES, LANES), LANES)
        cols = pl.ds(pl.multiple_of(z * part + n * LANES, LANES), LANES)
        for c in range(lane_blocks):
            rows = slice(c * LANES, (c + 1) * LANES)
            w1t[at, rows] = win[rows, cols].astype(f32).T.astype(bf16)
        return carry

    lax.fori_loop(0, part // LANES, turn, 0)

    def clear(i, carry):
        at = pl.ds(pl.multiple_of(i * 16, 16), 16)
        for k in range(SIDE):
            g_in[k, at, :] = jnp.zeros((16, width), f32)
            g_out[k, at, :] = jnp.zeros((16, width), f32)
        return carry

    lax.fori_loop(0, part // 16, clear, 0)
    load_wout.wait()
    w2_rows = pl.ds(pl.multiple_of(z * part, part), part)

    def grads(slot, rows):
        t = tok[slot, rows, :]
        u = ups[slot, rows, :]
        act, slope = gelu_parts(dot_nt(w1t[...], t))
        ht[...] = act.astype(bf16)
        hgt[...] = (slope * dot_nt(wout[w2_rows, :], u)).astype(bf16)
        g_out[slot] = g_out[slot] + jnp.dot(ht[...], u, preferred_element_type=f32)
        g_in[slot] = g_in[slot] + jnp.dot(hgt[...], t, preferred_element_type=f32)

    def own_step(q, carry):
        for c in range(2):
            for copy in dispatch(q, c):
                copy.wait_recv()
            for copy in first_hop(q, c):
                copy.start()
        grads(0, chip_rows(q - 1))
        return carry

    lax.fori_loop(1, SIDE, own_step, 0)
    grads(0, chip_rows(SIDE - 1))

    tile = 512
    rows_all = tok.shape[1]
    half = rows_all // 2

    def forward(n, carry):
        cols = pl.ds(pl.multiple_of(n * tile, tile), tile)
        for r in range(2):
            rows = slice(r * half, (r + 1) * half)
            pre = jnp.dot(tok[0, rows, :], win[:, cols], preferred_element_type=f32)
            hid = gelu_only(pre).astype(bf16)
            more = jnp.dot(hid, wout[cols, :], preferred_element_type=f32)
            acc[rows, :] = acc[rows, :] + more
        return carry

    acc[...] = jnp.zeros_like(acc)
    lax.fori_loop(0, win.shape[1] // tile, forward, 0)

    def round_out(i, carry):
        at = pl.ds(pl.multiple_of(i * cap, cap), cap)
        eout[at, :] = acc[at, :].astype(bf16)
        return carry

    lax.fori_loop(0, rows_all // cap, round_out, 0)

    def back(k):
        there = lax.rem(me + k, 8)
        return pltpu.make_async_remote_copy(
            src_ref=eout.at[pl.ds(pl.multiple_of(there * cap, cap), cap)],
            dst_ref=ret.at[me],
            send_sem=e_send.at[k],
            recv_sem=e_recv.at[k],
            **to(dp, there),
        )

    for k in range(1, 8):
        back(k).start()
    back_own = pltpu.make_async_copy(eout.at[own_rows], ret.at[me], loc_sem.at[0])
    back_own.start()

    def near_step(q, carry):
        for c in range(2):
            for copy in first_hop(q, c):
                copy.wait_recv()
        for copy in second_hop(q):
            copy.start()
        grads(1, chip_rows(q))
        grads(3, chip_rows(q))
        return carry

    lax.fori_loop(0, SIDE, near_step, 0)

    for k in range(1, 8):
        back(k).wait_recv()
    back_own.wait()
    for p in range(8):
        cols = slice(p * cap, (p + 1) * cap)
        for b in range(toks // LANES):
            at = slice(b * LANES, (b + 1) * LANES)
            slots = lax.broadcasted_iota(jnp.int32, (LANES, cap), 1).astype(f32) + float(p * cap)
            pick[at, cols] = (slots == code_cols[at, :]).astype(f32).astype(bf16)
    picked = jnp.dot(pick[...], ret[...].reshape(8 * cap, width), preferred_element_type=f32)
    for c in range(lane_blocks):
        cols = slice(c * LANES, (c + 1) * LANES)
        combined[:, cols] = (gate_cols[...] * picked[:, cols]).astype(bf16)

    def far_step(q, carry):
        for copy in second_hop(q):
            copy.wait_recv()
        grads(2, chip_rows(q))
        return carry

    lax.fori_loop(0, SIDE, far_step, 0)

    for p, s in enumerate(gram_sums((g_in, g_out), part)):
        gz_out[p : p + 1, :] = jnp.sum(s, axis=0, keepdims=True)
    sums_z = []
    for i in range(1, SIDE):
        copy = pltpu.make_async_remote_copy(
            src_ref=gz_out,
            dst_ref=gz_got.at[SIDE - i],
            send_sem=gz_send.at[SIDE - i],
            recv_sem=gz_recv.at[SIDE - i],
            **to(at_zy(i, 0), me),
        )
        copy.start()
        sums_z.append(copy)
    total = [gz_out[p : p + 1, :] for p in range(len(PAIRS))]
    for copy in sums_z:
        copy.wait_recv()
    for i in range(1, SIDE):
        for p, (a, b) in enumerate(PAIRS):
            q = SLOT[tuple(sorted(((a + i) % SIDE, (b + i) % SIDE)))]
            total[q] = total[q] + gz_got[i, p : p + 1, :]
    total = [jnp.sum(t, axis=1, keepdims=True) for t in total]
    w = tree_weights(lambda a, b: total[SLOT[(a, b)]])

    rows_out = seg_out.shape[0]
    rows_in = seg_in.shape[0]

    def send_out(j):
        k = (SIDE - j) % SIDE
        return [
            pltpu.make_async_remote_copy(
                src_ref=src.at[j],
                dst_ref=dst.at[k],
                send_sem=yo_send.at[h, k],
                recv_sem=yo_recv.at[h, k],
                **to(at_zy(0, j), me),
            )
            for h, (src, dst) in enumerate(((q_out, rq_out), (f_out, rf_out)))
        ]

    def send_in(i, j):
        n = i * SIDE + j
        k = (SIDE - j) % SIDE
        m = lax.rem(SIDE - i, SIDE) * SIDE + k
        return [
            pltpu.make_async_remote_copy(
                src_ref=src.at[n],
                dst_ref=dst.at[k, z],
                send_sem=yi_send.at[h, m],
                recv_sem=yi_recv.at[h, m],
                **to(at_zy(i, j), me),
            )
            for h, (src, dst) in enumerate(((q_in, rq_in), (f_in, rf_in)))
        ]

    for j in (1, 3, 2):
        rows = pl.ds(pl.multiple_of(lax.rem(y + j, SIDE) * rows_out, 8), rows_out)
        for c in range(lane_blocks):
            cols = slice(c * LANES, (c + 1) * LANES)
            v = w[0] * g_out[0, rows, cols] + w[1] * g_out[1, rows, cols]
            v = v + w[2] * g_out[2, rows, cols] + w[3] * g_out[3, rows, cols]
            q_out[j, :, cols], f_out[j, c : c + 1, :] = encode(v)
        for copy in send_out(j):
            copy.start()

    def mix_in(n, carry):
        cols = pl.ds(pl.multiple_of(n * LANES, LANES), LANES)
        for m in range(part // LANES):
            at = slice(m * LANES, (m + 1) * LANES)
            v = w[0] * g_in[0, at, cols] + w[1] * g_in[1, at, cols]
            v = v + w[2] * g_in[2, at, cols] + w[3] * g_in[3, at, cols]
            acc[cols, at] = v.T
        return carry

    lax.fori_loop(0, width // LANES, mix_in, 0)

    def block_rows(i, j):
        return pl.ds(pl.multiple_of(at_zy(i, j) * rows_in, 8), rows_in)

    for j in (1, 3, 2, 0):

        def code_in(i, carry, j=j):
            rows = block_rows(i, j)
            for c in range(lane_blocks):
                cols = slice(c * LANES, (c + 1) * LANES)
                codes, factor = encode(acc[rows, cols])
                q_in[i * SIDE + j, :, cols] = codes
                f_in[i * SIDE + j, c : c + 1, :] = factor
            for copy in send_in(i, j):
                copy.start()
            return carry

        lax.fori_loop(0 if j else 1, SIDE, code_in, 0)

    g_in[0, pl.ds(pl.multiple_of(z * rows_in, 8), rows_in), :] = acc[block_rows(0, 0), :]
    base = y * rows_out

    def mix_own(n, carry):
        rows = pl.ds(pl.multiple_of(base + n * 16, 16), 16)
        v = w[0] * g_out[0, rows, :] + w[1] * g_out[1, rows, :]
        v = v + w[2] * g_out[2, rows, :] + w[3] * g_out[3, rows, :]
        g_out[0, pl.ds(pl.multiple_of(n * 16, 16), 16), :] = v
        return carry

    lax.fori_loop(0, rows_out // 16, mix_own, 0)

    for k in (0, 3, 1, 2):
        j = (SIDE - k) % SIDE

        def decode_in(i, carry, j=j, k=k):
            for copy in send_in(i, j):
                copy.wait_recv()
            there = lax.rem(z + SIDE - i, SIDE)
            rows = pl.ds(pl.multiple_of(there * rows_in, 8), rows_in)
            for c in range(lane_blocks):
                cols = slice(c * LANES, (c + 1) * LANES)
                codes = rq_in[k, there, :, cols].astype(jnp.int32).astype(f32)
                g_in[k, rows, cols] = codes * rf_in[k, there, c : c + 1, :]
            return carry

        if k:
            for copy in send_out(j):
                copy.wait_recv()
            for c in range(lane_blocks):
                cols = slice(c * LANES, (c + 1) * LANES)
                codes = rq_out[k, :, cols].astype(jnp.int32).astype(f32)
                g_out[k, :rows_out, cols] = codes * rf_out[k, c : c + 1, :]
        lax.fori_loop(0 if k else 1, SIDE, decode_in, 0)

    for p, s in enumerate(gram_sums((g_in, g_out), rows_out)):
        gy_out[p : p + 1, :] = jnp.sum(s, axis=0, keepdims=True)
    sums_y = []
    for i in range(SIDE):
        for j in range(SIDE):
            if i or j:
                k = (SIDE - i) % SIDE * SIDE + (SIDE - j) % SIDE
                copy = pltpu.make_async_remote_copy(
                    src_ref=gy_out,
                    dst_ref=gy_got.at[k],
                    send_sem=gy_send.at[k],
                    recv_sem=gy_recv.at[k],
                    **to(at_zy(i, j), me),
                )
                copy.start()
                sums_y.append(copy)
    total = [gy_out[p : p + 1, :] for p in range(len(PAIRS))]
    for copy in sums_y:
        copy.wait_recv()
    for j in range(SIDE):
        for i in range(SIDE):
            if i or j:
                for p, (a, b) in enumerate(PAIRS):
                    q = SLOT[tuple(sorted(((a + j) % SIDE, (b + j) % SIDE)))]
                    total[q] = total[q] + gy_got[i * SIDE + j, p : p + 1, :]
    total = [jnp.sum(t, axis=1, keepdims=True) for t in total]
    v = tree_weights(lambda a, b: total[SLOT[(a, b)]])
    for i in range(SIDE):
        at = slice(i * rows_in, (i + 1) * rows_in)
        seg_in[:, i * part : (i + 1) * part] = (v[0] * g_in[0, at, :] + v[1] * g_in[1, at, :]) + (
            v[2] * g_in[2, at, :] + v[3] * g_in[3, at, :]
        )
        seg_out[at, :] = (v[0] * g_out[0, at, :] + v[1] * g_out[1, at, :]) + (
            v[2] * g_out[2, at, :] + v[3] * g_out[3, at, :]
        )

    def drain(q, carry):
        for copy in first_hop(q, 0) + first_hop(q, 1) + second_hop(q):
            copy.wait_send()
        return carry

    lax.fori_loop(0, SIDE, drain, 0)

    def drain_dispatch(q, carry):
        for copy in dispatch(q, 0) + dispatch(q, 1):
            copy.wait_send()
        return carry

    lax.fori_loop(1, SIDE, drain_dispatch, 0)
    for copy in dispatch(0, 1):
        copy.wait_send()
    for k in range(1, 8):
        back(k).wait_send()
    for j in range(SIDE):

        def drain_in(i, carry, j=j):
            for copy in send_in(i, j):
                copy.wait_send()
            return carry

        lax.fori_loop(0 if j else 1, SIDE, drain_in, 0)
        if j:
            for copy in send_out(j):
                copy.wait_send()
    for copy in sums_z + sums_y:
        copy.wait_send()


def expert_step(assigned, gate, tokens, cotangent, w_in, w_out):
    f32 = jnp.float32
    bf16 = jnp.bfloat16
    i16 = jnp.int16
    experts = 8
    toks, width = tokens.shape
    cap = 2 * toks // experts
    rows = experts * cap
    side = SIDE
    part = w_in.shape[1] // side
    any_space = pl.BlockSpec(memory_space=pl.ANY)
    vmem = pl.BlockSpec(memory_space=pltpu.VMEM)
    rows_in = width // (side * side)
    rows_out = part // side
    dma = pltpu.SemaphoreType.DMA
    return pl.pallas_call(
        kernel,
        out_shape=(
            jax.ShapeDtypeStruct((toks, width), bf16),
            jax.ShapeDtypeStruct((rows_in, side * part), f32),
            jax.ShapeDtypeStruct((rows_out, width), f32),
        ),
        in_specs=[vmem, vmem, vmem, vmem, any_space, any_space],
        out_specs=(vmem, vmem, vmem),
        scratch_shapes=[
            pltpu.VMEM((side, rows, width), bf16),
            pltpu.VMEM((side, rows, width), bf16),
            pltpu.VMEM(w_in.shape, bf16),
            pltpu.VMEM(w_out.shape, bf16),
            pltpu.VMEM((part, width), bf16),
            pltpu.VMEM((side, part, width), f32),
            pltpu.VMEM((side, part, width), f32),
            pltpu.VMEM((part, 2 * cap), bf16),
            pltpu.VMEM((part, 2 * cap), bf16),
            pltpu.VMEM((side, 2 * cap, width), bf16),
            pltpu.VMEM((side, 2 * cap, width), bf16),
            pltpu.VMEM((toks, width), bf16),
            pltpu.VMEM((toks, LANES), f32),
            pltpu.VMEM((toks, LANES), f32),
            pltpu.VMEM((rows, width), bf16),
            pltpu.VMEM((experts, cap, width), bf16),
            pltpu.VMEM((toks, rows), bf16),
            pltpu.VMEM((rows, width), f32),
            pltpu.VMEM((side * side, rows_in, part), i16),
            pltpu.VMEM((side, rows_out, width), i16),
            pltpu.VMEM((side, side, rows_in, part), i16),
            pltpu.VMEM((side, rows_out, width), i16),
            pltpu.VMEM((side * side, 8, LANES), f32),
            pltpu.VMEM((side, 8, LANES), f32),
            pltpu.VMEM((side, side, 8, LANES), f32),
            pltpu.VMEM((side, 8, LANES), f32),
            pltpu.VMEM((16, LANES), f32),
            pltpu.VMEM((side, 16, LANES), f32),
            pltpu.VMEM((16, LANES), f32),
            pltpu.VMEM((side * side, 16, LANES), f32),
            dma((2,)),
            dma((1,)),
            dma((2, 8)),
            dma((2, 8)),
            dma((2, 2, 8)),
            dma((2, 2, 8)),
            dma((2, side)),
            dma((2, side)),
            dma((8,)),
            dma((8,)),
            dma((side,)),
            dma((side,)),
            dma((2, side)),
            dma((2, side)),
            dma((2, side * side)),
            dma((2, side * side)),
            dma((side * side,)),
            dma((side * side,)),
        ],
        compiler_params=pltpu.CompilerParams(
            collective_id=0, has_side_effects=True, vmem_limit_bytes=67_000_000
        ),
        name="expert_step",
    )(assigned, gate, tokens, cotangent, w_in, w_out)


def body(
    tokens,
    assigned,
    gate_prob,
    cotangent,
    weight_in,
    weight_out,
    moment_in,
    moment_out,
    second_in,
    second_out,
):
    f32 = jnp.float32
    replicas = lax.axis_size("dp")
    self_index = lax.axis_index("dp")
    toks, width = tokens.shape
    hidden_width = weight_in.shape[2]
    w_first = weight_in[0]
    w_second = weight_out[0]
    combined, seg_first, seg_second = expert_step(
        assigned.reshape(1, toks), gate_prob.reshape(1, toks), tokens, cotangent, w_first, w_second
    )
    rows_first = width // replicas
    rows_second = hidden_width // replicas
    own_first = lax.dynamic_slice_in_dim(w_first, self_index * rows_first, rows_first, 0).astype(
        f32
    )
    own_second = lax.dynamic_slice_in_dim(
        w_second, self_index * rows_second, rows_second, 0
    ).astype(f32)
    new_w_first, new_m_first, new_v_first = adam_update(
        seg_first, own_first, moment_in[0], second_in[0]
    )
    new_w_second, new_m_second, new_v_second = adam_update(
        seg_second, own_second, moment_out[0], second_out[0]
    )
    return (
        combined,
        new_w_first[None],
        new_w_second[None],
        new_m_first[None],
        new_m_second[None],
        new_v_first[None],
        new_v_second[None],
    )


def solution(mesh):
    return jax.shard_map(
        body,
        mesh=mesh,
        in_specs=(
            P(("dp", "expert"), None),
            P(("dp", "expert"), None),
            P(("dp", "expert"), None),
            P(("dp", "expert"), None),
            P("expert", None, None),
            P("expert", None, None),
            P("expert", "dp", None),
            P("expert", "dp", None),
            P("expert", "dp", None),
            P("expert", "dp", None),
        ),
        out_specs=(
            P(("dp", "expert"), None),
            P("expert", "dp", None),
            P("expert", "dp", None),
            P("expert", "dp", None),
            P("expert", "dp", None),
            P("expert", "dp", None),
            P("expert", "dp", None),
        ),
        check_vma=False,
    )
```

time: 210 us -> 167 us (0.80)
  Pallas kernels: 192 us -> 159 us
  matrix products: 6.62 us -> 0 us
  local copies, waits for them, and re-layouts: 3.16 us -> 0.88 us
    pallas_call x1, Pallas kernels: 192 us -> 159 us  [expert_step(): pl.pallas_call(kernel, out_shape=(jax.ShapeDtypeStruct((toks, width), bf1...]
    dot_general x3 -> x0, matrix products: 6.62 us -> none  [the longest x2 4.5 us: placed(): out = jnp.dot(table, rows, preferred_element_type=f32).astype(bf16)]
    dynamic_slice x2 -> x0, local copies, waits for them, and re-layouts: 2.89 us -> none  [body(): w1t = lax.dynamic_slice_in_dim(w_first, z_index * part, part, 1).T]
where the time goes in v3:
time: 167 us
  Pallas kernels  159 us (95%)
  other arithmetic  6.3 us (4%)
    pallas_call x1, Pallas kernels, expert_step(): pl.pallas_call(kernel, out_shape=(jax.ShapeDtypeStruct((toks, width), bf1...  159 us

profile of v3, /device:TPU:0, one launch (start us, length us, event | category | flops | bytes accessed | tf_op | source)
XLA Modules:
  0.0 167.1 jit_solution(12635541829354044972)
XLA Ops:
  0.6 159.2 %expert_step.1 = (bf16[512,768]{1,0:T(8,128)(2,1)}, f32[48,3072]{1,0:T(8,128)}, f32[192,768]{1,0:T(8,128)}) custom-call(s32[1,512]{1,0:T(1,128)} %bitcast.48, f32[1,512]{1,0:T(1,128)} %bitcast.49, bf16[512,768]{1,0:T(8,128)(2,1)} %tokens.1, bf16[512,768]{1,0:T(8,128)(2,1)} %cotangent.1, bf16[768,3072]{1,0:T(8,128)(2,1)} %bitcast.46, bf16[3072,768]{1,0:T(8,128)(2,1)} %bitcast.47), custom_call_target="tpu_custom_call" | custom-call | tf_op jit(solution)/shard_map/expert_step/pallas_call | solution.py:595
  159.9 0.0 copy-start
  159.9 3.2 %fusion.7 = (f32[1,48,3072]{2,1,0:T(8,128)}, f32[1,48,3072]{2,1,0:T(8,128)}, f32[1,48,3072]{2,1,0:T(8,128)}) fusion(f32[48,3072]{1,0:T(8,128)} %get-tuple-element.11, f32[1,48,3072]{2,1,0:T(8,128)} %param.18, f32[1,48,3072]{2,1,0:T(8,128)} %param.16, bf16[1,768,3072]{2,1,0:T(8,128)(2,1)} %param.14, s32[]{:T(128)S(6)} %select_n.6), kind=kLoop, calls=%fused_computation.13 | loop fusion | flops 2064384 | bytes 3833860 | tf_op jit(solution)/shard_map/broadcast_in_dim | solution.py:703
  163.1 3.1 %fusion.6 = (f32[1,192,768]{2,1,0:T(8,128)}, f32[1,192,768]{2,1,0:T(8,128)}, f32[1,192,768]{2,1,0:T(8,128)}) fusion(f32[192,768]{1,0:T(8,128)} %get-tuple-element.12, f32[1,192,768]{2,1,0:T(8,128)} %param.19, f32[1,192,768]{2,1,0:T(8,128)} %param.17, bf16[1,3072,768]{2,1,0:T(8,128)(2,1)} %param.15, s32[]{:T(128)S(6)} %select_n.7), kind=kLoop, calls=%fused_computation.12 | loop fusion | flops 2064384 | bytes 3833860 | tf_op jit(solution)/shard_map/broadcast_in_dim | solution.py:704
  166.2 0.0 copy-done
  166.2 0.9 copy.18
Async XLA Ops:
  159.9 6.3 %copy-start = (bf16[512,768]{1,0:T(8,128)(2,1)S(1)}, bf16[512,768]{1,0:T(8,128)(2,1)}, u32[]{:S(2)}) copy-start(bf16[512,768]{1,0:T(8,128)(2,1)} %get-tuple-element.26) | copy-start | bytes 2359300

commit v4 on v3

--- a/solution.py
+++ b/solution.py
@@ -8,6 +8,7 @@
 eps_adasum = 1e-06
 SIDE = 4
 LANES = 128
+SPLIT = 512
 MESH = pl.DeviceIdType.MESH
 PAIRS = [(a, b) for a in range(SIDE) for b in range(a, SIDE)]
 SLOT = {pair: k for k, pair in enumerate(PAIRS)}
@@ -106,11 +107,13 @@
     sent_t,
     sent_u,
     scaled,
+    raw,
+    place_own,
+    places,
     code_cols,
     gate_cols,
     eout,
     ret,
-    pick,
     acc,
     q_in,
     q_out,
@@ -128,6 +131,12 @@
     loc_sem,
     d_send,
     d_recv,
+    rz_send,
+    rz_recv,
+    rfar_send,
+    rfar_recv,
+    b_send,
+    b_recv,
     zf_send,
     zf_recv,
     far_send,
@@ -183,6 +192,7 @@
     ).astype(f32)
     rank = jnp.dot(hot.astype(bf16), earlier.astype(bf16), preferred_element_type=f32)
     place = (named * cap).astype(f32) + jnp.sum(rank * hot, axis=0, keepdims=True)
+    place_own[...] = jnp.broadcast_to(place, place_own.shape)
     for b in range(toks // LANES):
         at = slice(b * LANES, (b + 1) * LANES)
         code_cols[at, :] = columns_of(place[:, at])
@@ -198,10 +208,13 @@
     def chip_rows(q):
         return pl.ds(pl.multiple_of(lax.rem(x + SIDE - (q ^ (q >> 1)), SIDE) * chunk, chunk), chunk)
 
-    def place_rows(q):
+    def table_of(q, places_row):
         base = (chip_at(q) * chunk).astype(f32)
         slots = lax.broadcasted_iota(jnp.int32, (chunk, toks), 0).astype(f32) + base
-        table = (slots == place).astype(f32).astype(bf16)
+        return (slots == places_row).astype(f32).astype(bf16)
+
+    def place_rows(q):
+        table = table_of(q, place)
         sent_t[q] = jnp.dot(table, tokens[...], preferred_element_type=f32).astype(bf16)
         sent_u[q] = jnp.dot(table, scaled[...], preferred_element_type=f32).astype(bf16)
 
@@ -220,8 +233,8 @@
 
     def along_z(buf, slot, to_slot, rows, step, send, recv):
         return pltpu.make_async_remote_copy(
-            src_ref=buf.at[slot, rows],
-            dst_ref=buf.at[to_slot, rows],
+            src_ref=buf.at[slot, rows, :SPLIT],
+            dst_ref=buf.at[to_slot, rows, :SPLIT],
             send_sem=send,
             recv_sem=recv,
             **to(at_zy(step, 0), me),
@@ -244,11 +257,52 @@
             along_z(ups, 1, 2, rows, 3, far_send.at[1, q], far_recv.at[1, q]),
         ]
 
+    def raw_hop(what, way):
+        src, dst, base = (
+            (tokens.at[:, SPLIT:], raw, 0),
+            (scaled.at[:, SPLIT:], raw, 3),
+            (place_own, places, 0),
+        )[what]
+        return pltpu.make_async_remote_copy(
+            src_ref=src,
+            dst_ref=dst.at[base + (0 if way else 2)],
+            send_sem=rz_send.at[way, what],
+            recv_sem=rz_recv.at[way, what],
+            **to(at_zy(3 if way else 1, 0), me),
+        )
+
+    def raw_far(what):
+        buf, source, there = ((raw, 2, 1), (raw, 3, 4), (places, 2, 1))[what]
+        return pltpu.make_async_remote_copy(
+            src_ref=buf.at[source],
+            dst_ref=buf.at[there],
+            send_sem=rfar_send.at[what],
+            recv_sem=rfar_recv.at[what],
+            **to(at_zy(3 if what == 1 else 1, 0), me),
+        )
+
+    def raw_dispatch(slot, q, c):
+        there = lax.rem(core + c, 2)
+        cols = slice((slot - 1) * (width - SPLIT), slot * (width - SPLIT))
+        return [
+            pltpu.make_async_remote_copy(
+                src_ref=src.at[q, pl.ds(pl.multiple_of(there * cap, cap), cap), cols],
+                dst_ref=dst.at[slot, own_rows, SPLIT:],
+                send_sem=b_send.at[slot - 1, h, 2 * q + c],
+                recv_sem=b_recv.at[slot - 1, h, 2 * q + c],
+                **to(dp, chip_at(q) * 2 + there),
+            )
+            for h, (src, dst) in enumerate(((sent_t, tok), (sent_u, ups)))
+        ]
+
+    pl.semaphore_wait(barrier, 7 + SIDE * SIDE - 1)
+    for what in (0, 1, 2):
+        for way in range(2):
+            raw_hop(what, way).start()
     place_rows(0)
     half_rows = pl.ds(pl.multiple_of(core * cap, cap), cap)
     tok[0, own_rows, :] = sent_t[0, half_rows, :]
     ups[0, own_rows, :] = sent_u[0, half_rows, :]
-    pl.semaphore_wait(barrier, 7 + SIDE * SIDE - 1)
     for copy in dispatch(0, 1) + first_hop(0, 0):
         copy.start()
 
@@ -296,6 +350,12 @@
         g_out[slot] = g_out[slot] + jnp.dot(ht[...], u, preferred_element_type=f32)
         g_in[slot] = g_in[slot] + jnp.dot(hgt[...], t, preferred_element_type=f32)
 
+    for what in range(3):
+        for way in range(2):
+            raw_hop(what, way).wait_recv()
+    for what in range(3):
+        raw_far(what).start()
+
     def own_step(q, carry):
         for c in range(2):
             for copy in dispatch(q, c):
@@ -307,6 +367,47 @@
 
     lax.fori_loop(1, SIDE, own_step, 0)
     grads(0, chip_rows(SIDE - 1))
+
+    def place_raw(slot, q):
+        cols = slice((slot - 1) * (width - SPLIT), slot * (width - SPLIT))
+        table = table_of(q, places[slot - 1, 0:1, :])
+        for sent, base in ((sent_t, 0), (sent_u, 3)):
+            rows = jnp.dot(table, raw[base + slot - 1], preferred_element_type=f32)
+            sent[q, :, cols] = rows.astype(bf16)
+
+    for slot in (1, 3, 2):
+        if slot == 2:
+            for what in range(3):
+                raw_far(what).wait_recv()
+        cols = slice((slot - 1) * (width - SPLIT), slot * (width - SPLIT))
+        if slot == 1:
+            for copy in dispatch(0, 1):
+                copy.wait_send()
+        place_raw(slot, 0)
+        tok[slot, own_rows, SPLIT:] = sent_t[0, half_rows, cols]
+        ups[slot, own_rows, SPLIT:] = sent_u[0, half_rows, cols]
+        for copy in raw_dispatch(slot, 0, 1):
+            copy.start()
+
+        def raw_step(q, carry, slot=slot):
+            if slot == 1:
+                for copy in dispatch(q, 0) + dispatch(q, 1):
+                    copy.wait_send()
+            place_raw(slot, q)
+            for copy in raw_dispatch(slot, q, 0) + raw_dispatch(slot, q, 1):
+                copy.start()
+            return carry
+
+        lax.fori_loop(1, SIDE, raw_step, 0)
+
+    def raw_arrived(slot, q):
+        @pl.when(q > 0)
+        def _():
+            for copy in raw_dispatch(slot, q, 0):
+                copy.wait_recv()
+
+        for copy in raw_dispatch(slot, q, 1):
+            copy.wait_recv()
 
     tile = 512
     rows_all = tok.shape[1]
@@ -353,6 +454,8 @@
                 copy.wait_recv()
         for copy in second_hop(q):
             copy.start()
+        raw_arrived(1, q)
+        raw_arrived(3, q)
         grads(1, chip_rows(q))
         grads(3, chip_rows(q))
         return carry
@@ -362,13 +465,19 @@
     for k in range(1, 8):
         back(k).wait_recv()
     back_own.wait()
-    for p in range(8):
-        cols = slice(p * cap, (p + 1) * cap)
+    for what in range(3):
+        raw_far(what).wait_send()
+    picked = jnp.zeros((toks, width), f32)
+    for p in range(SIDE):
         for b in range(toks // LANES):
             at = slice(b * LANES, (b + 1) * LANES)
-            slots = lax.broadcasted_iota(jnp.int32, (LANES, cap), 1).astype(f32) + float(p * cap)
-            pick[at, cols] = (slots == code_cols[at, :]).astype(f32).astype(bf16)
-    picked = jnp.dot(pick[...], ret[...].reshape(8 * cap, width), preferred_element_type=f32)
+            for h in range(2):
+                first = float((2 * p + h) * cap)
+                slots = lax.broadcasted_iota(jnp.int32, (LANES, cap), 1).astype(f32) + first
+                hit = (slots == code_cols[at, :]).astype(f32).astype(bf16)
+                raw[p, at, h * cap : (h + 1) * cap] = hit
+        rows = ret[2 * p : 2 * p + 2].reshape(chunk, width)
+        picked = picked + jnp.dot(raw[p], rows, preferred_element_type=f32)
     for c in range(lane_blocks):
         cols = slice(c * LANES, (c + 1) * LANES)
         combined[:, cols] = (gate_cols[...] * picked[:, cols]).astype(bf16)
@@ -376,6 +485,7 @@
     def far_step(q, carry):
         for copy in second_hop(q):
             copy.wait_recv()
+        raw_arrived(2, q)
         grads(2, chip_rows(q))
         return carry
 
@@ -552,14 +662,19 @@
 
     lax.fori_loop(0, SIDE, drain, 0)
 
-    def drain_dispatch(q, carry):
-        for copy in dispatch(q, 0) + dispatch(q, 1):
+    for slot in range(1, SIDE):
+        for copy in raw_dispatch(slot, 0, 1):
             copy.wait_send()
-        return carry
-
-    lax.fori_loop(1, SIDE, drain_dispatch, 0)
-    for copy in dispatch(0, 1):
-        copy.wait_send()
+
+        def drain_raw(q, carry, slot=slot):
+            for copy in raw_dispatch(slot, q, 0) + raw_dispatch(slot, q, 1):
+                copy.wait_send()
+            return carry
+
+        lax.fori_loop(1, SIDE, drain_raw, 0)
+    for what in range(3):
+        for way in range(2):
+            raw_hop(what, way).wait_send()
     for k in range(1, 8):
         back(k).wait_send()
     for j in range(SIDE):
@@ -614,11 +729,13 @@
             pltpu.VMEM((side, 2 * cap, width), bf16),
             pltpu.VMEM((side, 2 * cap, width), bf16),
             pltpu.VMEM((toks, width), bf16),
+            pltpu.VMEM((2 * (side - 1), toks, width - SPLIT), bf16),
+            pltpu.VMEM((8, toks), f32),
+            pltpu.VMEM((side - 1, 8, toks), f32),
             pltpu.VMEM((toks, LANES), f32),
             pltpu.VMEM((toks, LANES), f32),
             pltpu.VMEM((rows, width), bf16),
             pltpu.VMEM((experts, cap, width), bf16),
-            pltpu.VMEM((toks, rows), bf16),
             pltpu.VMEM((rows, width), f32),
             pltpu.VMEM((side * side, rows_in, part), i16),
             pltpu.VMEM((side, rows_out, width), i16),
@@ -636,6 +753,12 @@
             dma((1,)),
             dma((2, 8)),
             dma((2, 8)),
+            dma((2, 3)),
+            dma((2, 3)),
+            dma((3,)),
+            dma((3,)),
+            dma((side - 1, 2, 8)),
+            dma((side - 1, 2, 8)),
             dma((2, 2, 8)),
             dma((2, 2, 8)),
             dma((2, side)),

time: 167 us -> 165 us (0.988); the launches traced: 167 us -> 163 us
  Pallas kernels: 159 us -> 155 us
    pallas_call x1, Pallas kernels: 159 us -> 155 us  [expert_step(): pl.pallas_call(kernel, out_shape=(jax.ShapeDtypeStruct((toks, width), bf1...]
where the time goes in v4:
time: 165 us; the launch traced here: 163 us
  Pallas kernels  155 us (94%)
  other arithmetic  6.3 us (4%)
    pallas_call x1, Pallas kernels, expert_step(): pl.pallas_call(kernel, out_shape=(jax.ShapeDtypeStruct((toks, width), bf1...  155 us

profile of v4, /device:TPU:0, one launch (start us, length us, event | category | flops | bytes accessed | tf_op | source)
XLA Modules:
  0.0 163.1 jit_solution(15734912251472482689)
XLA Ops:
  0.6 155.2 %expert_step.1 = (bf16[512,768]{1,0:T(8,128)(2,1)}, f32[48,3072]{1,0:T(8,128)}, f32[192,768]{1,0:T(8,128)}) custom-call(s32[1,512]{1,0:T(1,128)} %bitcast.48, f32[1,512]{1,0:T(1,128)} %bitcast.49, bf16[512,768]{1,0:T(8,128)(2,1)} %tokens.1, bf16[512,768]{1,0:T(8,128)(2,1)} %cotangent.1, bf16[768,3072]{1,0:T(8,128)(2,1)} %bitcast.46, bf16[3072,768]{1,0:T(8,128)(2,1)} %bitcast.47), custom_call_target="tpu_custom_call" | custom-call | tf_op jit(solution)/shard_map/expert_step/pallas_call | solution.py:710
  155.9 0.0 copy-start
  155.9 3.2 %fusion.7 = (f32[1,48,3072]{2,1,0:T(8,128)}, f32[1,48,3072]{2,1,0:T(8,128)}, f32[1,48,3072]{2,1,0:T(8,128)}) fusion(f32[48,3072]{1,0:T(8,128)} %get-tuple-element.11, f32[1,48,3072]{2,1,0:T(8,128)} %param.18, f32[1,48,3072]{2,1,0:T(8,128)} %param.16, bf16[1,768,3072]{2,1,0:T(8,128)(2,1)} %param.14, s32[]{:T(128)S(6)} %select_n.6), kind=kLoop, calls=%fused_computation.13 | loop fusion | flops 2064384 | bytes 3833860 | tf_op jit(solution)/shard_map/broadcast_in_dim | solution.py:826
  159.1 3.1 %fusion.6 = (f32[1,192,768]{2,1,0:T(8,128)}, f32[1,192,768]{2,1,0:T(8,128)}, f32[1,192,768]{2,1,0:T(8,128)}) fusion(f32[192,768]{1,0:T(8,128)} %get-tuple-element.12, f32[1,192,768]{2,1,0:T(8,128)} %param.19, f32[1,192,768]{2,1,0:T(8,128)} %param.17, bf16[1,3072,768]{2,1,0:T(8,128)(2,1)} %param.15, s32[]{:T(128)S(6)} %select_n.7), kind=kLoop, calls=%fused_computation.12 | loop fusion | flops 2064384 | bytes 3833860 | tf_op jit(solution)/shard_map/broadcast_in_dim | solution.py:827
  162.2 0.0 copy-done
  162.2 0.9 copy.18
Async XLA Ops:
  155.9 6.3 %copy-start = (bf16[512,768]{1,0:T(8,128)(2,1)S(1)}, bf16[512,768]{1,0:T(8,128)(2,1)}, u32[]{:S(2)}) copy-start(bf16[512,768]{1,0:T(8,128)(2,1)} %get-tuple-element.26) | copy-start | bytes 2359300

commit v5 on v4

--- a/solution.py
+++ b/solution.py
@@ -350,6 +350,31 @@
         g_out[slot] = g_out[slot] + jnp.dot(ht[...], u, preferred_element_type=f32)
         g_in[slot] = g_in[slot] + jnp.dot(hgt[...], t, preferred_element_type=f32)
 
+    tile = part
+
+    def forward(rows):
+        acc[rows, :] = jnp.zeros((chunk, width), f32)
+
+        def step(n, carry):
+            cols = pl.ds(pl.multiple_of(n * tile, tile), tile)
+            pre = jnp.dot(tok[0, rows, :], win[:, cols], preferred_element_type=f32)
+            hid = gelu_only(pre).astype(bf16)
+            acc[rows, :] = acc[rows, :] + jnp.dot(hid, wout[cols, :], preferred_element_type=f32)
+            return carry
+
+        lax.fori_loop(0, win.shape[1] // tile, step, 0)
+        eout[rows, :] = acc[rows, :].astype(bf16)
+
+    def back(q, c):
+        there = lax.rem(x + SIDE - (q ^ (q >> 1)), SIDE) * 2 + lax.rem(core + c, 2)
+        return pltpu.make_async_remote_copy(
+            src_ref=eout.at[pl.ds(pl.multiple_of(there * cap, cap), cap)],
+            dst_ref=ret.at[me],
+            send_sem=e_send.at[2 * q + c],
+            recv_sem=e_recv.at[2 * q + c],
+            **to(dp, there),
+        )
+
     for what in range(3):
         for way in range(2):
             raw_hop(what, way).wait_recv()
@@ -363,10 +388,10 @@
             for copy in first_hop(q, c):
                 copy.start()
         grads(0, chip_rows(q - 1))
+        forward(chip_rows(q - 1))
         return carry
 
     lax.fori_loop(1, SIDE, own_step, 0)
-    grads(0, chip_rows(SIDE - 1))
 
     def place_raw(slot, q):
         cols = slice((slot - 1) * (width - SPLIT), slot * (width - SPLIT))
@@ -400,6 +425,9 @@
 
         lax.fori_loop(1, SIDE, raw_step, 0)
 
+    grads(0, chip_rows(SIDE - 1))
+    forward(chip_rows(SIDE - 1))
+
     def raw_arrived(slot, q):
         @pl.when(q > 0)
         def _():
@@ -409,42 +437,10 @@
         for copy in raw_dispatch(slot, q, 1):
             copy.wait_recv()
 
-    tile = 512
-    rows_all = tok.shape[1]
-    half = rows_all // 2
-
-    def forward(n, carry):
-        cols = pl.ds(pl.multiple_of(n * tile, tile), tile)
-        for r in range(2):
-            rows = slice(r * half, (r + 1) * half)
-            pre = jnp.dot(tok[0, rows, :], win[:, cols], preferred_element_type=f32)
-            hid = gelu_only(pre).astype(bf16)
-            more = jnp.dot(hid, wout[cols, :], preferred_element_type=f32)
-            acc[rows, :] = acc[rows, :] + more
-        return carry
-
-    acc[...] = jnp.zeros_like(acc)
-    lax.fori_loop(0, win.shape[1] // tile, forward, 0)
-
-    def round_out(i, carry):
-        at = pl.ds(pl.multiple_of(i * cap, cap), cap)
-        eout[at, :] = acc[at, :].astype(bf16)
-        return carry
-
-    lax.fori_loop(0, rows_all // cap, round_out, 0)
-
-    def back(k):
-        there = lax.rem(me + k, 8)
-        return pltpu.make_async_remote_copy(
-            src_ref=eout.at[pl.ds(pl.multiple_of(there * cap, cap), cap)],
-            dst_ref=ret.at[me],
-            send_sem=e_send.at[k],
-            recv_sem=e_recv.at[k],
-            **to(dp, there),
-        )
-
-    for k in range(1, 8):
-        back(k).start()
+    for q in range(SIDE):
+        for c in range(2):
+            if q or c:
+                back(q, c).start()
     back_own = pltpu.make_async_copy(eout.at[own_rows], ret.at[me], loc_sem.at[0])
     back_own.start()
 
@@ -461,26 +457,6 @@
         return carry
 
     lax.fori_loop(0, SIDE, near_step, 0)
-
-    for k in range(1, 8):
-        back(k).wait_recv()
-    back_own.wait()
-    for what in range(3):
-        raw_far(what).wait_send()
-    picked = jnp.zeros((toks, width), f32)
-    for p in range(SIDE):
-        for b in range(toks // LANES):
-            at = slice(b * LANES, (b + 1) * LANES)
-            for h in range(2):
-                first = float((2 * p + h) * cap)
-                slots = lax.broadcasted_iota(jnp.int32, (LANES, cap), 1).astype(f32) + first
-                hit = (slots == code_cols[at, :]).astype(f32).astype(bf16)
-                raw[p, at, h * cap : (h + 1) * cap] = hit
-        rows = ret[2 * p : 2 * p + 2].reshape(chunk, width)
-        picked = picked + jnp.dot(raw[p], rows, preferred_element_type=f32)
-    for c in range(lane_blocks):
-        cols = slice(c * LANES, (c + 1) * LANES)
-        combined[:, cols] = (gate_cols[...] * picked[:, cols]).astype(bf16)
 
     def far_step(q, carry):
         for copy in second_hop(q):
@@ -595,6 +571,28 @@
         return carry
 
     lax.fori_loop(0, rows_out // 16, mix_own, 0)
+
+    for q in range(SIDE):
+        for c in range(2):
+            if q or c:
+                back(q, c).wait_recv()
+    back_own.wait()
+    for what in range(3):
+        raw_far(what).wait_send()
+    picked = jnp.zeros((toks, width), f32)
+    for p in range(SIDE):
+        for b in range(toks // LANES):
+            at = slice(b * LANES, (b + 1) * LANES)
+            for h in range(2):
+                first = float((2 * p + h) * cap)
+                slots = lax.broadcasted_iota(jnp.int32, (LANES, cap), 1).astype(f32) + first
+                hit = (slots == code_cols[at, :]).astype(f32).astype(bf16)
+                raw[p, at, h * cap : (h + 1) * cap] = hit
+        rows = ret[2 * p : 2 * p + 2].reshape(chunk, width)
+        picked = picked + jnp.dot(raw[p], rows, preferred_element_type=f32)
+    for c in range(lane_blocks):
+        cols = slice(c * LANES, (c + 1) * LANES)
+        combined[:, cols] = (gate_cols[...] * picked[:, cols]).astype(bf16)
 
     for k in (0, 3, 1, 2):
         j = (SIDE - k) % SIDE
@@ -675,8 +673,10 @@
     for what in range(3):
         for way in range(2):
             raw_hop(what, way).wait_send()
-    for k in range(1, 8):
-        back(k).wait_send()
+    for q in range(SIDE):
+        for c in range(2):
+            if q or c:
+                back(q, c).wait_send()
     for j in range(SIDE):
 
         def drain_in(i, carry, j=j):

time: 165 us -> 152 us (0.921); the launches traced: 163 us -> 152 us
  Pallas kernels: 155 us -> 144 us
    pallas_call x1, Pallas kernels: 155 us -> 144 us  [expert_step(): pl.pallas_call(kernel, out_shape=(jax.ShapeDtypeStruct((toks, width), bf1...]
where the time goes in v5:
time: 152 us
  Pallas kernels  144 us (95%)
  other arithmetic  6.3 us (4%)
    pallas_call x1, Pallas kernels, expert_step(): pl.pallas_call(kernel, out_shape=(jax.ShapeDtypeStruct((toks, width), bf1...  144 us
    broadcast_in_dim x1, other arithmetic, body(): new_v_first[None]  3.19 us
    broadcast_in_dim x1, other arithmetic, body(): new_v_second[None]  3.11 us

profile of v5, /device:TPU:0, one launch (start us, length us, event | category | flops | bytes accessed | tf_op | source)
XLA Modules:
  0.0 152.2 jit_solution(11045832693295747545)
XLA Ops:
  0.6 144.4 %expert_step.1 = (bf16[512,768]{1,0:T(8,128)(2,1)}, f32[48,3072]{1,0:T(8,128)}, f32[192,768]{1,0:T(8,128)}) custom-call(s32[1,512]{1,0:T(1,128)} %bitcast.48, f32[1,512]{1,0:T(1,128)} %bitcast.49, bf16[512,768]{1,0:T(8,128)(2,1)} %tokens.1, bf16[512,768]{1,0:T(8,128)(2,1)} %cotangent.1, bf16[768,3072]{1,0:T(8,128)(2,1)} %bitcast.46, bf16[3072,768]{1,0:T(8,128)(2,1)} %bitcast.47), custom_call_target="tpu_custom_call" | custom-call | tf_op jit(solution)/shard_map/expert_step/pallas_call | solution.py:710
  145.0 0.0 copy-start
  145.0 3.2 %fusion.7 = (f32[1,48,3072]{2,1,0:T(8,128)}, f32[1,48,3072]{2,1,0:T(8,128)}, f32[1,48,3072]{2,1,0:T(8,128)}) fusion(f32[48,3072]{1,0:T(8,128)} %get-tuple-element.11, f32[1,48,3072]{2,1,0:T(8,128)} %param.18, f32[1,48,3072]{2,1,0:T(8,128)} %param.16, bf16[1,768,3072]{2,1,0:T(8,128)(2,1)} %param.14, s32[]{:T(128)S(6)} %select_n.6), kind=kLoop, calls=%fused_computation.13 | loop fusion | flops 2064384 | bytes 3833860 | tf_op jit(solution)/shard_map/broadcast_in_dim | solution.py:826
  148.2 3.1 %fusion.6 = (f32[1,192,768]{2,1,0:T(8,128)}, f32[1,192,768]{2,1,0:T(8,128)}, f32[1,192,768]{2,1,0:T(8,128)}) fusion(f32[192,768]{1,0:T(8,128)} %get-tuple-element.12, f32[1,192,768]{2,1,0:T(8,128)} %param.19, f32[1,192,768]{2,1,0:T(8,128)} %param.17, bf16[1,3072,768]{2,1,0:T(8,128)(2,1)} %param.15, s32[]{:T(128)S(6)} %select_n.7), kind=kLoop, calls=%fused_computation.12 | loop fusion | flops 2064384 | bytes 3833860 | tf_op jit(solution)/shard_map/broadcast_in_dim | solution.py:827
  151.3 0.0 copy-done
  151.3 0.9 copy.18
Async XLA Ops:
  145.0 6.3 %copy-start = (bf16[512,768]{1,0:T(8,128)(2,1)S(1)}, bf16[512,768]{1,0:T(8,128)(2,1)}, u32[]{:S(2)}) copy-start(bf16[512,768]{1,0:T(8,128)(2,1)} %get-tuple-element.26) | copy-start | bytes 2359300

commit v6 on v5

--- a/solution.py
+++ b/solution.py
@@ -8,10 +8,12 @@
 eps_adasum = 1e-06
 SIDE = 4
 LANES = 128
-SPLIT = 512
+PANELS = 3
 MESH = pl.DeviceIdType.MESH
 PAIRS = [(a, b) for a in range(SIDE) for b in range(a, SIDE)]
 SLOT = {pair: k for k, pair in enumerate(PAIRS)}
+FAR = [pair for pair in PAIRS if 2 in pair]
+NEAR = [pair for pair in PAIRS if 2 not in pair]
 
 
 def adam_update(grad, weight, moment, second):
@@ -67,8 +69,9 @@
     return codes, most * (1.0 / 32767.0)
 
 
-def gram_sums(refs, rows):
+def gram_sums(refs, rows, pairs):
     width = refs[0].shape[2]
+    used = sorted({k for pair in pairs for k in pair})
 
     def step(i, sums):
         sums = list(sums)
@@ -76,13 +79,13 @@
         for ref in refs:
             for c in range(width // LANES):
                 cols = slice(c * LANES, (c + 1) * LANES)
-                v = [ref[k, at, cols] for k in range(SIDE)]
-                for p, (a, b) in enumerate(PAIRS):
+                v = {k: ref[k, at, cols] for k in used}
+                for p, (a, b) in enumerate(pairs):
                     sums[p] = sums[p] + v[a] * v[b]
         return tuple(sums)
 
     zero = jnp.zeros((8, LANES), jnp.float32)
-    return lax.fori_loop(0, rows // 8, step, (zero,) * len(PAIRS))
+    return lax.fori_loop(0, rows // 8, step, (zero,) * len(pairs))
 
 
 def kernel(
@@ -107,11 +110,10 @@
     sent_t,
     sent_u,
     scaled,
+    last,
     raw,
     place_own,
     places,
-    code_cols,
-    gate_cols,
     eout,
     ret,
     acc,
@@ -163,6 +165,7 @@
     part = w1t.shape[0]
     toks, width = tokens.shape
     lane_blocks = width // LANES
+    panel = width // PANELS
     own_rows = pl.ds(pl.multiple_of(me * cap, cap), cap)
 
     def at_zy(i, j):
@@ -183,6 +186,25 @@
         for j in range(SIDE):
             if i or j:
                 pl.semaphore_signal(barrier, inc=1, **to(at_zy(i, j), me))
+
+    def raw_hop(what, way):
+        src, dst, base = (
+            (last, raw, 0),
+            (scaled.at[PANELS - 1], raw, 3),
+            (place_own, places, 0),
+        )[what]
+        return pltpu.make_async_remote_copy(
+            src_ref=src,
+            dst_ref=dst.at[base + (0 if way else 2)],
+            send_sem=rz_send.at[way, what],
+            recv_sem=rz_recv.at[way, what],
+            **to(at_zy(3 if way else 1, 0), me),
+        )
+
+    last[...] = tokens[:, width - panel :]
+    pl.semaphore_wait(barrier, 7 + SIDE * SIDE - 1)
+    for way in range(2):
+        raw_hop(0, way).start()
 
     named = assigned[...]
     hot = (lax.broadcasted_iota(jnp.int32, (16, toks), 0) == named).astype(f32)
@@ -195,12 +217,12 @@
     place_own[...] = jnp.broadcast_to(place, place_own.shape)
     for b in range(toks // LANES):
         at = slice(b * LANES, (b + 1) * LANES)
-        code_cols[at, :] = columns_of(place[:, at])
         column = columns_of(gate[:, at])
-        gate_cols[at, :] = column
         for c in range(lane_blocks):
             cols = slice(c * LANES, (c + 1) * LANES)
-            scaled[at, cols] = (column * cotangent[at, cols].astype(f32)).astype(bf16)
+            value = (column * cotangent[at, cols].astype(f32)).astype(bf16)
+            start = c * LANES % panel
+            scaled[c * LANES // panel, at, start : start + LANES] = value
 
     def chip_at(q):
         return lax.rem(x + (q ^ (q >> 1)), SIDE)
@@ -213,17 +235,26 @@
         slots = lax.broadcasted_iota(jnp.int32, (chunk, toks), 0).astype(f32) + base
         return (slots == places_row).astype(f32).astype(bf16)
 
+    def panels_of(p):
+        return slice(p * panel, (p + 1) * panel)
+
+    def joined(buf, slot, rows):
+        return jnp.concatenate([buf[slot, p, rows, :] for p in range(PANELS)], axis=1)
+
     def place_rows(q):
         table = table_of(q, place)
-        sent_t[q] = jnp.dot(table, tokens[...], preferred_element_type=f32).astype(bf16)
-        sent_u[q] = jnp.dot(table, scaled[...], preferred_element_type=f32).astype(bf16)
+        for p in range(PANELS):
+            rows = jnp.dot(table, tokens[:, panels_of(p)], preferred_element_type=f32)
+            sent_t[p, q] = rows.astype(bf16)
+            rows = jnp.dot(table, scaled[p], preferred_element_type=f32)
+            sent_u[p, q] = rows.astype(bf16)
 
     def dispatch(q, c):
         there = lax.rem(core + c, 2)
         return [
             pltpu.make_async_remote_copy(
-                src_ref=src.at[q, pl.ds(pl.multiple_of(there * cap, cap), cap)],
-                dst_ref=dst.at[0, own_rows],
+                src_ref=src.at[:, q, pl.ds(pl.multiple_of(there * cap, cap), cap)],
+                dst_ref=dst.at[0, :, own_rows],
                 send_sem=d_send.at[h, 2 * q + c],
                 recv_sem=d_recv.at[h, 2 * q + c],
                 **to(dp, chip_at(q) * 2 + there),
@@ -233,8 +264,8 @@
 
     def along_z(buf, slot, to_slot, rows, step, send, recv):
         return pltpu.make_async_remote_copy(
-            src_ref=buf.at[slot, rows, :SPLIT],
-            dst_ref=buf.at[to_slot, rows, :SPLIT],
+            src_ref=buf.at[slot, : PANELS - 1, rows],
+            dst_ref=buf.at[to_slot, : PANELS - 1, rows],
             send_sem=send,
             recv_sem=recv,
             **to(at_zy(step, 0), me),
@@ -257,20 +288,6 @@
             along_z(ups, 1, 2, rows, 3, far_send.at[1, q], far_recv.at[1, q]),
         ]
 
-    def raw_hop(what, way):
-        src, dst, base = (
-            (tokens.at[:, SPLIT:], raw, 0),
-            (scaled.at[:, SPLIT:], raw, 3),
-            (place_own, places, 0),
-        )[what]
-        return pltpu.make_async_remote_copy(
-            src_ref=src,
-            dst_ref=dst.at[base + (0 if way else 2)],
-            send_sem=rz_send.at[way, what],
-            recv_sem=rz_recv.at[way, what],
-            **to(at_zy(3 if way else 1, 0), me),
-        )
-
     def raw_far(what):
         buf, source, there = ((raw, 2, 1), (raw, 3, 4), (places, 2, 1))[what]
         return pltpu.make_async_remote_copy(
@@ -283,11 +300,10 @@
 
     def raw_dispatch(slot, q, c):
         there = lax.rem(core + c, 2)
-        cols = slice((slot - 1) * (width - SPLIT), slot * (width - SPLIT))
         return [
             pltpu.make_async_remote_copy(
-                src_ref=src.at[q, pl.ds(pl.multiple_of(there * cap, cap), cap), cols],
-                dst_ref=dst.at[slot, own_rows, SPLIT:],
+                src_ref=src.at[slot - 1, q, pl.ds(pl.multiple_of(there * cap, cap), cap)],
+                dst_ref=dst.at[slot, PANELS - 1, own_rows],
                 send_sem=b_send.at[slot - 1, h, 2 * q + c],
                 recv_sem=b_recv.at[slot - 1, h, 2 * q + c],
                 **to(dp, chip_at(q) * 2 + there),
@@ -295,14 +311,14 @@
             for h, (src, dst) in enumerate(((sent_t, tok), (sent_u, ups)))
         ]
 
-    pl.semaphore_wait(barrier, 7 + SIDE * SIDE - 1)
-    for what in (0, 1, 2):
+    for what in (1, 2):
         for way in range(2):
             raw_hop(what, way).start()
     place_rows(0)
     half_rows = pl.ds(pl.multiple_of(core * cap, cap), cap)
-    tok[0, own_rows, :] = sent_t[0, half_rows, :]
-    ups[0, own_rows, :] = sent_u[0, half_rows, :]
+    for p in range(PANELS):
+        tok[0, p, own_rows, :] = sent_t[p, 0, half_rows, :]
+        ups[0, p, own_rows, :] = sent_u[p, 0, half_rows, :]
     for copy in dispatch(0, 1) + first_hop(0, 0):
         copy.start()
 
@@ -342,8 +358,8 @@
     w2_rows = pl.ds(pl.multiple_of(z * part, part), part)
 
     def grads(slot, rows):
-        t = tok[slot, rows, :]
-        u = ups[slot, rows, :]
+        t = joined(tok, slot, rows)
+        u = joined(ups, slot, rows)
         act, slope = gelu_parts(dot_nt(w1t[...], t))
         ht[...] = act.astype(bf16)
         hgt[...] = (slope * dot_nt(wout[w2_rows, :], u)).astype(bf16)
@@ -357,7 +373,7 @@
 
         def step(n, carry):
             cols = pl.ds(pl.multiple_of(n * tile, tile), tile)
-            pre = jnp.dot(tok[0, rows, :], win[:, cols], preferred_element_type=f32)
+            pre = jnp.dot(joined(tok, 0, rows), win[:, cols], preferred_element_type=f32)
             hid = gelu_only(pre).astype(bf16)
             acc[rows, :] = acc[rows, :] + jnp.dot(hid, wout[cols, :], preferred_element_type=f32)
             return carry
@@ -388,29 +404,31 @@
             for copy in first_hop(q, c):
                 copy.start()
         grads(0, chip_rows(q - 1))
-        forward(chip_rows(q - 1))
+
+        @pl.when(q < SIDE - 1)
+        def _():
+            forward(chip_rows(q - 1))
+
         return carry
 
     lax.fori_loop(1, SIDE, own_step, 0)
 
     def place_raw(slot, q):
-        cols = slice((slot - 1) * (width - SPLIT), slot * (width - SPLIT))
         table = table_of(q, places[slot - 1, 0:1, :])
         for sent, base in ((sent_t, 0), (sent_u, 3)):
             rows = jnp.dot(table, raw[base + slot - 1], preferred_element_type=f32)
-            sent[q, :, cols] = rows.astype(bf16)
+            sent[slot - 1, q] = rows.astype(bf16)
 
     for slot in (1, 3, 2):
         if slot == 2:
             for what in range(3):
                 raw_far(what).wait_recv()
-        cols = slice((slot - 1) * (width - SPLIT), slot * (width - SPLIT))
         if slot == 1:
             for copy in dispatch(0, 1):
                 copy.wait_send()
         place_raw(slot, 0)
-        tok[slot, own_rows, SPLIT:] = sent_t[0, half_rows, cols]
-        ups[slot, own_rows, SPLIT:] = sent_u[0, half_rows, cols]
+        tok[slot, PANELS - 1, own_rows, :] = sent_t[slot - 1, 0, half_rows, :]
+        ups[slot, PANELS - 1, own_rows, :] = sent_u[slot - 1, 0, half_rows, :]
         for copy in raw_dispatch(slot, 0, 1):
             copy.start()
 
@@ -426,7 +444,6 @@
         lax.fori_loop(1, SIDE, raw_step, 0)
 
     grads(0, chip_rows(SIDE - 1))
-    forward(chip_rows(SIDE - 1))
 
     def raw_arrived(slot, q):
         @pl.when(q > 0)
@@ -437,7 +454,7 @@
         for copy in raw_dispatch(slot, q, 1):
             copy.wait_recv()
 
-    for q in range(SIDE):
+    for q in range(2):
         for c in range(2):
             if q or c:
                 back(q, c).start()
@@ -458,6 +475,13 @@
 
     lax.fori_loop(0, SIDE, near_step, 0)
 
+    def z_sums(pairs):
+        for pair, s in zip(pairs, gram_sums((g_in, g_out), part, pairs)):
+            p = SLOT[pair]
+            gz_out[p : p + 1, :] = jnp.sum(s, axis=0, keepdims=True)
+
+    z_sums(NEAR)
+
     def far_step(q, carry):
         for copy in second_hop(q):
             copy.wait_recv()
@@ -467,8 +491,7 @@
 
     lax.fori_loop(0, SIDE, far_step, 0)
 
-    for p, s in enumerate(gram_sums((g_in, g_out), part)):
-        gz_out[p : p + 1, :] = jnp.sum(s, axis=0, keepdims=True)
+    z_sums(FAR)
     sums_z = []
     for i in range(1, SIDE):
         copy = pltpu.make_async_remote_copy(
@@ -572,27 +595,13 @@
 
     lax.fori_loop(0, rows_out // 16, mix_own, 0)
 
-    for q in range(SIDE):
-        for c in range(2):
-            if q or c:
-                back(q, c).wait_recv()
-    back_own.wait()
-    for what in range(3):
-        raw_far(what).wait_send()
-    picked = jnp.zeros((toks, width), f32)
-    for p in range(SIDE):
-        for b in range(toks // LANES):
-            at = slice(b * LANES, (b + 1) * LANES)
-            for h in range(2):
-                first = float((2 * p + h) * cap)
-                slots = lax.broadcasted_iota(jnp.int32, (LANES, cap), 1).astype(f32) + first
-                hit = (slots == code_cols[at, :]).astype(f32).astype(bf16)
-                raw[p, at, h * cap : (h + 1) * cap] = hit
-        rows = ret[2 * p : 2 * p + 2].reshape(chunk, width)
-        picked = picked + jnp.dot(raw[p], rows, preferred_element_type=f32)
-    for c in range(lane_blocks):
-        cols = slice(c * LANES, (c + 1) * LANES)
-        combined[:, cols] = (gate_cols[...] * picked[:, cols]).astype(bf16)
+    def late_step(q, carry):
+        forward(chip_rows(q))
+        for copy in (back(q, 0), back(q, 1)):
+            copy.start()
+        return carry
+
+    lax.fori_loop(2, SIDE, late_step, 0)
 
     for k in (0, 3, 1, 2):
         j = (SIDE - k) % SIDE
@@ -617,7 +626,7 @@
                 g_out[k, :rows_out, cols] = codes * rf_out[k, c : c + 1, :]
         lax.fori_loop(0 if k else 1, SIDE, decode_in, 0)
 
-    for p, s in enumerate(gram_sums((g_in, g_out), rows_out)):
+    for p, s in enumerate(gram_sums((g_in, g_out), rows_out, PAIRS)):
         gy_out[p : p + 1, :] = jnp.sum(s, axis=0, keepdims=True)
     sums_y = []
     for i in range(SIDE):
@@ -633,6 +642,30 @@
                 )
                 copy.start()
                 sums_y.append(copy)
+    for q in range(SIDE):
+        for c in range(2):
+            if q or c:
+                back(q, c).wait_recv()
+    back_own.wait()
+    for what in range(3):
+        raw_far(what).wait_send()
+    for b in range(toks // LANES):
+        at = slice(b * LANES, (b + 1) * LANES)
+        code = columns_of(place_own[0:1, at])
+        for n in range(2 * SIDE):
+            slots = lax.broadcasted_iota(jnp.int32, (LANES, cap), 1).astype(f32) + float(n * cap)
+            hit = (slots == code).astype(f32).astype(bf16)
+            raw[n // 2, at, n % 2 * cap : (n % 2 + 1) * cap] = hit
+    picked = jnp.zeros((toks, width), f32)
+    for p in range(SIDE):
+        rows = ret[2 * p : 2 * p + 2].reshape(chunk, width)
+        picked = picked + jnp.dot(raw[p], rows, preferred_element_type=f32)
+    for b in range(toks // LANES):
+        at = slice(b * LANES, (b + 1) * LANES)
+        column = columns_of(gate[:, at])
+        for c in range(lane_blocks):
+            cols = slice(c * LANES, (c + 1) * LANES)
+            combined[at, cols] = (column * picked[at, cols]).astype(bf16)
     total = [gy_out[p : p + 1, :] for p in range(len(PAIRS))]
     for copy in sums_y:
         copy.wait_recv()
@@ -717,8 +750,8 @@
         in_specs=[vmem, vmem, vmem, vmem, any_space, any_space],
         out_specs=(vmem, vmem, vmem),
         scratch_shapes=[
-            pltpu.VMEM((side, rows, width), bf16),
-            pltpu.VMEM((side, rows, width), bf16),
+            pltpu.VMEM((side, PANELS, rows, width // PANELS), bf16),
+            pltpu.VMEM((side, PANELS, rows, width // PANELS), bf16),
             pltpu.VMEM(w_in.shape, bf16),
             pltpu.VMEM(w_out.shape, bf16),
             pltpu.VMEM((part, width), bf16),
@@ -726,14 +759,13 @@
             pltpu.VMEM((side, part, width), f32),
             pltpu.VMEM((part, 2 * cap), bf16),
             pltpu.VMEM((part, 2 * cap), bf16),
-            pltpu.VMEM((side, 2 * cap, width), bf16),
-            pltpu.VMEM((side, 2 * cap, width), bf16),
-            pltpu.VMEM((toks, width), bf16),
-            pltpu.VMEM((2 * (side - 1), toks, width - SPLIT), bf16),
+            pltpu.VMEM((PANELS, side, 2 * cap, width // PANELS), bf16),
+            pltpu.VMEM((PANELS, side, 2 * cap, width // PANELS), bf16),
+            pltpu.VMEM((PANELS, toks, width // PANELS), bf16),
+            pltpu.VMEM((toks, width // PANELS), bf16),
+            pltpu.VMEM((2 * (side - 1), toks, width // PANELS), bf16),
             pltpu.VMEM((8, toks), f32),
             pltpu.VMEM((side - 1, 8, toks), f32),
-            pltpu.VMEM((toks, LANES), f32),
-            pltpu.VMEM((toks, LANES), f32),
             pltpu.VMEM((rows, width), bf16),
             pltpu.VMEM((experts, cap, width), bf16),
             pltpu.VMEM((rows, width), f32),
@@ -781,6 +813,37 @@
     )(assigned, gate, tokens, cotangent, w_in, w_out)
 
 
+def adam_kernel(index, *refs):
+    for grad, weight, moment, second, new_weight, new_moment, new_second in (
+        refs[0:4] + refs[8:11],
+        refs[4:8] + refs[11:14],
+    ):
+        out = adam_update(grad[...], weight[0].astype(jnp.float32), moment[0], second[0])
+        new_weight[0], new_moment[0], new_second[0] = out
+
+
+def adam_step(index, first, second):
+    steps = 3
+    in_specs, out_specs, out_shape = [], [], []
+    for grad, weight, moment, _ in (first, second):
+        rows, cols = grad.shape
+        own = (1, rows // steps, cols)
+        state = pl.BlockSpec(own, lambda i, index: (0, i, 0))
+        in_specs.append(pl.BlockSpec(own[1:], lambda i, index: (i, 0)))
+        in_specs.append(pl.BlockSpec(own, lambda i, index: (0, index[0] * steps + i, 0)))
+        in_specs += [state, state]
+        out_specs += [state] * 3
+        out_shape += [jax.ShapeDtypeStruct(moment.shape, jnp.float32)] * 3
+    return pl.pallas_call(
+        adam_kernel,
+        out_shape=out_shape,
+        grid_spec=pltpu.PrefetchScalarGridSpec(
+            num_scalar_prefetch=1, grid=(steps,), in_specs=in_specs, out_specs=out_specs
+        ),
+        name="adam_step",
+    )(index, *first, *second)
+
+
 def body(
     tokens,
     assigned,
@@ -793,38 +856,26 @@
     second_in,
     second_out,
 ):
-    f32 = jnp.float32
-    replicas = lax.axis_size("dp")
     self_index = lax.axis_index("dp")
-    toks, width = tokens.shape
-    hidden_width = weight_in.shape[2]
+    toks = tokens.shape[0]
     w_first = weight_in[0]
     w_second = weight_out[0]
     combined, seg_first, seg_second = expert_step(
         assigned.reshape(1, toks), gate_prob.reshape(1, toks), tokens, cotangent, w_first, w_second
     )
-    rows_first = width // replicas
-    rows_second = hidden_width // replicas
-    own_first = lax.dynamic_slice_in_dim(w_first, self_index * rows_first, rows_first, 0).astype(
-        f32
-    )
-    own_second = lax.dynamic_slice_in_dim(
-        w_second, self_index * rows_second, rows_second, 0
-    ).astype(f32)
-    new_w_first, new_m_first, new_v_first = adam_update(
-        seg_first, own_first, moment_in[0], second_in[0]
-    )
-    new_w_second, new_m_second, new_v_second = adam_update(
-        seg_second, own_second, moment_out[0], second_out[0]
+    new_w_first, new_m_first, new_v_first, new_w_second, new_m_second, new_v_second = adam_step(
+        self_index.reshape(1),
+        (seg_first, weight_in, moment_in, second_in),
+        (seg_second, weight_out, moment_out, second_out),
     )
     return (
         combined,
-        new_w_first[None],
-        new_w_second[None],
-        new_m_first[None],
-        new_m_second[None],
-        new_v_first[None],
-        new_v_second[None],
+        new_w_first,
+        new_w_second,
+        new_m_first,
+        new_m_second,
+        new_v_first,
+        new_v_second,
     )
 
 

time: 152 us -> 149 us (0.980)
  other arithmetic: 6.3 us -> 0 us
  Pallas kernels: 144 us -> 148 us
    broadcast_in_dim x2 -> x0, other arithmetic: 6.3 us -> none  [the longest x1 3.19 us: body(): new_v_first[None]]
    pallas_call x0 -> x1, Pallas kernels: none -> 5.16 us  [adam_step(): pl.pallas_call(adam_kernel, out_shape=out_shape, grid_spec=pltpu.Prefetch...]
    pallas_call x1, Pallas kernels: 144 us -> 142 us  [expert_step(): pl.pallas_call(kernel, out_shape=(jax.ShapeDtypeStruct((toks, width), bf1...]
where the time goes in v6:
time: 149 us
  Pallas kernels  148 us (99%)
    pallas_call x1, Pallas kernels, expert_step(): pl.pallas_call(kernel, out_shape=(jax.ShapeDtypeStruct((toks, width), bf1...  142 us
    pallas_call x1, Pallas kernels, adam_step(): pl.pallas_call(adam_kernel, out_shape=out_shape, grid_spec=pltpu.Prefetch...  5.16 us

profile of v6, /device:TPU:0, one launch (start us, length us, event | category | flops | bytes accessed | tf_op | source)
XLA Modules:
  0.0 149.1 jit_solution(1972635628123787722)
XLA Ops:
  0.6 142.4 %expert_step.1 = (bf16[512,768]{1,0:T(8,128)(2,1)}, f32[48,3072]{1,0:T(8,128)}, f32[192,768]{1,0:T(8,128)}) custom-call(s32[1,512]{1,0:T(1,128)} %bitcast.7, f32[1,512]{1,0:T(1,128)} %bitcast.8, bf16[512,768]{1,0:T(8,128)(2,1)} %tokens.1, bf16[512,768]{1,0:T(8,128)(2,1)} %cotangent.1, bf16[768,3072]{1,0:T(8,128)(2,1)} %bitcast.5, bf16[3072,768]{1,0:T(8,128)(2,1)} %bitcast.6), custom_call_target="tpu_custom_call" | custom-call | tf_op jit(solution)/shard_map/expert_step/pallas_call | solution.py:743
  143.1 0.0 copy-start
  143.1 5.2 %adam_step.1 = (f32[1,48,3072]{2,1,0:T(8,128)}, f32[1,48,3072]{2,1,0:T(8,128)}, f32[1,48,3072]{2,1,0:T(8,128)}, f32[1,192,768]{2,1,0:T(8,128)}, f32[1,192,768]{2,1,0:T(8,128)}, /*index=5*/f32[1,192,768]{2,1,0:T(8,128)}) custom-call(s32[1]{0:T(128)} %bitcast.4.index, f32[48,3072]{1,0:T(8,128)} %get-tuple-element.17.refs_0_, bf16[1,768,3072]{2,1,0:T(8,128)(2,1)} %refs_1_.1, ...), custom_call_target="tpu_custom_call" | custom-call | tf_op jit(solution)/shard_map/adam_step/pallas_call | solution.py:837
  148.3 0.0 copy-done
  148.3 0.9 copy.18
Async XLA Ops:
  143.1 5.2 %copy-start = (bf16[512,768]{1,0:T(8,128)(2,1)S(1)}, bf16[512,768]{1,0:T(8,128)(2,1)}, u32[]{:S(2)}) copy-start(bf16[512,768]{1,0:T(8,128)(2,1)} %get-tuple-element.32) | copy-start | bytes 2359300

commit v7 on v6

--- a/solution.py
+++ b/solution.py
@@ -603,8 +603,15 @@
 
     lax.fori_loop(2, SIDE, late_step, 0)
 
+    def y_sums(pairs):
+        for pair, s in zip(pairs, gram_sums((g_in, g_out), rows_out, pairs)):
+            p = SLOT[pair]
+            gy_out[p : p + 1, :] = jnp.sum(s, axis=0, keepdims=True)
+
     for k in (0, 3, 1, 2):
         j = (SIDE - k) % SIDE
+        if k == 2:
+            y_sums(NEAR)
 
         def decode_in(i, carry, j=j, k=k):
             for copy in send_in(i, j):
@@ -626,8 +633,7 @@
                 g_out[k, :rows_out, cols] = codes * rf_out[k, c : c + 1, :]
         lax.fori_loop(0 if k else 1, SIDE, decode_in, 0)
 
-    for p, s in enumerate(gram_sums((g_in, g_out), rows_out, PAIRS)):
-        gy_out[p : p + 1, :] = jnp.sum(s, axis=0, keepdims=True)
+    y_sums(FAR)
     sums_y = []
     for i in range(SIDE):
         for j in range(SIDE):
@@ -823,7 +829,7 @@
 
 
 def adam_step(index, first, second):
-    steps = 3
+    steps = 1
     in_specs, out_specs, out_shape = [], [], []
     for grad, weight, moment, _ in (first, second):
         rows, cols = grad.shape

time: 149 us -> 148 us (level)
  no operation moved by 1% of the time
where the time goes in v7:
time: 148 us
  Pallas kernels  147 us (99%)
    pallas_call x1, Pallas kernels, expert_step(): pl.pallas_call(kernel, out_shape=(jax.ShapeDtypeStruct((toks, width), bf1...  142 us
    pallas_call x1, Pallas kernels, adam_step(): pl.pallas_call(adam_kernel, out_shape=out_shape, grid_spec=pltpu.Prefetch...  4.46 us

profile of v7, /device:TPU:0, one launch (start us, length us, event | category | flops | bytes accessed | tf_op | source)
XLA Modules:
  0.0 148.2 jit_solution(13235625670551584067)
XLA Ops:
  0.6 142.2 %expert_step.1 = (bf16[512,768]{1,0:T(8,128)(2,1)}, f32[48,3072]{1,0:T(8,128)}, f32[192,768]{1,0:T(8,128)}) custom-call(s32[1,512]{1,0:T(1,128)} %bitcast.7, f32[1,512]{1,0:T(1,128)} %bitcast.8, bf16[512,768]{1,0:T(8,128)(2,1)} %tokens.1, bf16[512,768]{1,0:T(8,128)(2,1)} %cotangent.1, bf16[768,3072]{1,0:T(8,128)(2,1)} %bitcast.5, bf16[3072,768]{1,0:T(8,128)(2,1)} %bitcast.6), custom_call_target="tpu_custom_call" | custom-call | tf_op jit(solution)/shard_map/expert_step/pallas_call | solution.py:749
  142.9 0.0 copy-start
  142.9 4.5 %adam_step.1 = (f32[1,48,3072]{2,1,0:T(8,128)}, f32[1,48,3072]{2,1,0:T(8,128)}, f32[1,48,3072]{2,1,0:T(8,128)}, f32[1,192,768]{2,1,0:T(8,128)}, f32[1,192,768]{2,1,0:T(8,128)}, /*index=5*/f32[1,192,768]{2,1,0:T(8,128)}) custom-call(s32[1]{0:T(128)} %bitcast.4.index, f32[48,3072]{1,0:T(8,128)} %get-tuple-element.17.refs_0_, bf16[1,768,3072]{2,1,0:T(8,128)(2,1)} %refs_1_.1, ...), custom_call_target="tpu_custom_call" | custom-call | tf_op jit(solution)/shard_map/adam_step/pallas_call | solution.py:843
  147.3 0.0 copy-done
  147.3 0.9 copy.18
Async XLA Ops:
  142.9 4.5 %copy-start = (bf16[512,768]{1,0:T(8,128)(2,1)S(1)}, bf16[512,768]{1,0:T(8,128)(2,1)}, u32[]{:S(2)}) copy-start(bf16[512,768]{1,0:T(8,128)(2,1)} %get-tuple-element.32) | copy-start | bytes 2359300
